TPU v7x, 32 devices: a whole 2x2x4 slice. The times are simulated.
32 devices in a mesh: ctx: 8 (over z, y), fsdp: 4 (over x, core).
Axes of the slice: x: 2, y: 2, z: 4, core: 2. Of those that a mesh axis runs over, the one named last changes fastest.
Arguments:
- tokens: bfloat16 [4, 2048, 1024], P('fsdp', 'ctx'), may hold values from -6 to 6
- cotangent: bfloat16 [4, 2048, 1024], P('fsdp', 'ctx'), may hold values from -6 to 6
- block_order: int32 [4, 16], P('fsdp'), may hold values from 0 to 15, each once within a row
- w_qkv: bfloat16 [1024, 2048], P(('ctx', 'fsdp')), may hold values from -0.1875 to 0.1875
- w_out: bfloat16 [1024, 1024], P(None, ('ctx', 'fsdp')), may hold values from -3.5 to 3.5
- w_gate: bfloat16 [1024, 4608], P(('ctx', 'fsdp')), may hold values from -0.1875 to 0.1875
- w_up: bfloat16 [1024, 4608], P(('ctx', 'fsdp')), may hold values from -0.1875 to 0.1875
- w_down: bfloat16 [4608, 1024], P(None, ('ctx', 'fsdp')), may hold values from -0.09375 to 0.09375
- attn_gain: float32 [1024], replicated, may hold values from 0.1 to 1.9
- ffn_gain: float32 [1024], replicated, may hold values from 0.1 to 1.9
- query_gain: float32 [64], replicated, may hold values from 0.1 to 1.9
- key_gain: float32 [64], replicated, may hold values from 0.1 to 1.9
Outputs:
- block_out: bfloat16 [4, 2048, 1024], P('fsdp', 'ctx')
- input_grad: bfloat16 [4, 2048, 1024], P('fsdp', 'ctx')
- grad_qkv: float32 [1024, 2048], P(('ctx', 'fsdp'))
- grad_out: float32 [1024, 1024], P(None, ('ctx', 'fsdp'))
- grad_gate: float32 [1024, 4608], P(('ctx', 'fsdp'))
- grad_up: float32 [1024, 4608], P(('ctx', 'fsdp'))
- grad_down: float32 [4608, 1024], P(None, ('ctx', 'fsdp'))
- grad_attn_gain: float32 [1024], replicated
- grad_ffn_gain: float32 [1024], replicated
- grad_query_gain: float32 [64], replicated
- grad_key_gain: float32 [64], replicated
Inputs may be any that keep to these rules, and one draw needn't show every extreme that they name: Each row of block_order is a permutation: it names every block 0 to 15 exactly once, in no fixed pattern.
All inputs are finite; a program needn't handle non-finite values.
Results may differ from a plain program's by a relative error of at most 0.017.
Values may be sent and summed in bfloat16 or wider, within the bound.
A program may use at most 256 MiB of HBM per device.

v0:
```python
import jax
import jax.numpy as jnp
from jax import lax
from jax.sharding import PartitionSpec as P

HEADS = 16
KV_HEADS = 8
HD = 64
KBLOCK = 512


EPS = 1e-05
THETA = 1000000.0


def rms_norm(inputs, gain_row):
    return inputs * lax.rsqrt(jnp.mean(inputs * inputs, axis=-1, keepdims=True) + EPS) * gain_row


def rotary(inputs, cosines, sines):
    half_width = inputs.shape[-1] // 2
    turned = jnp.concatenate([-inputs[..., half_width:], inputs[..., :half_width]], axis=-1)
    return inputs * cosines + turned * sines


def angles(positions):
    exponent = jnp.arange(0, HD, 2).astype(jnp.float32) / HD
    inverse = jnp.power(THETA, -exponent)
    phases = positions.astype(jnp.float32)[:, None] * inverse[None, :]
    phases = jnp.concatenate([phases, phases], axis=-1)
    return (jnp.cos(phases)[:, None, :], jnp.sin(phases)[:, None, :])


def masked_scores(query_heads, key_block, query_spots, key_spots, scale):
    scores = (
        jnp.einsum("qngd,knd->ngqk", query_heads, key_block, preferred_element_type=jnp.float32)
        * scale
    )
    allowed = query_spots[:, None] >= key_spots[None, :]
    return jnp.where(allowed[None, None], scores, -1e30)


def body(
    tokens,
    cotangent,
    block_order,
    w_qkv,
    w_out,
    w_gate,
    w_up,
    w_down,
    attn_gain,
    ffn_gain,
    query_gain,
    key_gain,
):
    tok_rows = tokens.shape[1]
    model_width = tokens.shape[2]
    span_count = lax.axis_size("ctx")
    seq_rows = tok_rows * span_count
    half_rows = tok_rows // 2
    groups_per = HEADS // KV_HEADS
    scale = HD ** (-0.5)
    q_width = HEADS * HD
    kv_width = KV_HEADS * HD
    block_count = seq_rows // KBLOCK
    slot_order = block_order.reshape(-1)
    row_index = jnp.arange(seq_rows, dtype=jnp.int32)
    slot_of = row_index // half_rows
    picks = (slot_of[:, None] == jnp.arange(slot_order.shape[0], dtype=jnp.int32)[None, :]).astype(
        jnp.int32
    )
    key_spots = jnp.sum(picks * slot_order[None, :], axis=1) * half_rows + row_index % half_rows
    query_spots = lax.dynamic_slice_in_dim(key_spots, lax.axis_index("ctx") * tok_rows, tok_rows)
    cosines, sines = angles(query_spots)
    full_qkv, full_out, full_gate, full_up, full_down = (
        lax.all_gather(w_qkv, ("ctx", "fsdp"), axis=0, tiled=True),
        lax.all_gather(w_out, ("ctx", "fsdp"), axis=1, tiled=True),
        lax.all_gather(w_gate, ("ctx", "fsdp"), axis=0, tiled=True),
        lax.all_gather(w_up, ("ctx", "fsdp"), axis=0, tiled=True),
        lax.all_gather(w_down, ("ctx", "fsdp"), axis=1, tiled=True),
    )
    tok_f32 = tokens.reshape(tok_rows, model_width).astype(jnp.float32)
    normed, attn_pull = jax.vjp(rms_norm, tok_f32, attn_gain)
    normed_low = normed.astype(jnp.bfloat16)
    projected = jnp.dot(normed_low, full_qkv, preferred_element_type=jnp.float32)
    query_raw = projected[:, :q_width].reshape(tok_rows, HEADS, HD)
    key_raw = projected[:, q_width : q_width + kv_width].reshape(tok_rows, KV_HEADS, HD)
    value_low = projected[:, q_width + kv_width :].astype(jnp.bfloat16)

    def head_path(raw_heads, gain_row):
        return rotary(rms_norm(raw_heads, gain_row), cosines, sines)

    query_rot, query_pull = jax.vjp(head_path, query_raw, query_gain)
    key_rot, key_pull = jax.vjp(head_path, key_raw, key_gain)
    query_low = query_rot.astype(jnp.bfloat16).reshape(tok_rows, KV_HEADS, groups_per, HD)
    key_low = key_rot.astype(jnp.bfloat16).reshape(tok_rows, kv_width)
    keys_all, values_all = (
        lax.all_gather(key_low, "ctx", axis=0, tiled=True),
        lax.all_gather(value_low, "ctx", axis=0, tiled=True),
    )
    key_blocks = keys_all.reshape(block_count, KBLOCK, KV_HEADS, HD)
    value_blocks = values_all.reshape(block_count, KBLOCK, KV_HEADS, HD)
    spot_blocks = key_spots.reshape(block_count, KBLOCK)

    def max_pass(carry, block):
        running_top, running_sum = carry
        key_block, spot_block = block
        scores = masked_scores(query_low, key_block, query_spots, spot_block, scale)
        new_top = jnp.maximum(running_top, jnp.max(scores, axis=-1, keepdims=True))
        running_sum = running_sum * jnp.exp(running_top - new_top) + jnp.sum(
            jnp.exp(scores - new_top), axis=-1, keepdims=True
        )
        return ((new_top, running_sum), None)

    start_top = jnp.full((KV_HEADS, groups_per, tok_rows, 1), -1e30, jnp.float32)
    (top_final, sum_final), unused_one = lax.scan(
        max_pass, (start_top, jnp.zeros_like(start_top)), (key_blocks, spot_blocks)
    )
    log_total = top_final + jnp.log(sum_final)

    def value_pass(mixed, block):
        key_block, value_block, spot_block = block
        scores = masked_scores(query_low, key_block, query_spots, spot_block, scale)
        weights = jnp.exp(scores - log_total).astype(jnp.bfloat16)
        return (
            mixed
            + jnp.einsum(
                "ngqk,knd->qngd", weights, value_block, preferred_element_type=jnp.float32
            ),
            None,
        )

    start_mixed = jnp.zeros((tok_rows, KV_HEADS, groups_per, HD), jnp.float32)
    mixed, unused_two = lax.scan(value_pass, start_mixed, (key_blocks, value_blocks, spot_blocks))
    attended_low = mixed.reshape(tok_rows, q_width).astype(jnp.bfloat16)
    hidden = tok_f32 + jnp.dot(attended_low, full_out, preferred_element_type=jnp.float32)
    normed_two, ffn_pull = jax.vjp(rms_norm, hidden, ffn_gain)
    normed_two_low = normed_two.astype(jnp.bfloat16)
    gate_val = jnp.dot(normed_two_low, full_gate, preferred_element_type=jnp.float32)
    up_val = jnp.dot(normed_two_low, full_up, preferred_element_type=jnp.float32)

    def gated(gate_in, up_in):
        return jax.nn.silu(gate_in) * up_in

    activation, act_pull = jax.vjp(gated, gate_val, up_val)
    act_low = activation.astype(jnp.bfloat16)
    block_out = (hidden + jnp.dot(act_low, full_down, preferred_element_type=jnp.float32)).astype(
        jnp.bfloat16
    )
    cot_low = cotangent.reshape(tok_rows, model_width)
    grad_down = jnp.einsum("ti,tj->ij", act_low, cot_low, preferred_element_type=jnp.float32)
    act_grad = jnp.einsum("tj,ij->ti", cot_low, full_down, preferred_element_type=jnp.float32)
    gate_grad, up_grad = act_pull(act_grad)
    gate_low = gate_grad.astype(jnp.bfloat16)
    up_low = up_grad.astype(jnp.bfloat16)
    grad_gate = jnp.einsum(
        "ti,tj->ij", normed_two_low, gate_low, preferred_element_type=jnp.float32
    )
    grad_up = jnp.einsum("ti,tj->ij", normed_two_low, up_low, preferred_element_type=jnp.float32)
    normed_two_grad = jnp.einsum(
        "tj,ij->ti", gate_low, full_gate, preferred_element_type=jnp.float32
    )
    normed_two_grad = normed_two_grad + jnp.einsum(
        "tj,ij->ti", up_low, full_up, preferred_element_type=jnp.float32
    )
    hidden_back, ffn_gain_grad = ffn_pull(normed_two_grad)
    hidden_grad = cot_low.astype(jnp.float32) + hidden_back
    hidden_low = hidden_grad.astype(jnp.bfloat16)
    grad_out = jnp.einsum("ti,tj->ij", attended_low, hidden_low, preferred_element_type=jnp.float32)
    attended_grad = jnp.einsum(
        "tj,ij->ti", hidden_low, full_out, preferred_element_type=jnp.float32
    ).astype(jnp.bfloat16)
    grad_heads = attended_grad.reshape(tok_rows, KV_HEADS, groups_per, HD)
    diagonal = jnp.sum(grad_heads.astype(jnp.float32) * mixed, axis=-1)
    diagonal = jnp.transpose(diagonal, (1, 2, 0))[..., None]

    def grad_pass(query_acc, block):
        key_block, value_block, spot_block = block
        scores = masked_scores(query_low, key_block, query_spots, spot_block, scale)
        probs = jnp.exp(scores - log_total)
        prob_grad = jnp.einsum(
            "qngd,knd->ngqk", grad_heads, value_block, preferred_element_type=jnp.float32
        )
        score_low = (probs * (prob_grad - diagonal)).astype(jnp.bfloat16)
        value_grad = jnp.einsum(
            "ngqk,qngd->knd",
            probs.astype(jnp.bfloat16),
            grad_heads,
            preferred_element_type=jnp.float32,
        )
        key_grad = (
            jnp.einsum("ngqk,qngd->knd", score_low, query_low, preferred_element_type=jnp.float32)
            * scale
        )
        query_acc = (
            query_acc
            + jnp.einsum("ngqk,knd->qngd", score_low, key_block, preferred_element_type=jnp.float32)
            * scale
        )
        return (
            query_acc,
            (key_grad.reshape(KBLOCK, kv_width), value_grad.reshape(KBLOCK, kv_width)),
        )

    query_grad, (key_grads, value_grads) = lax.scan(
        grad_pass, jnp.zeros_like(start_mixed), (key_blocks, value_blocks, spot_blocks)
    )
    key_sum, value_sum = (
        lax.psum_scatter(
            key_grads.reshape(seq_rows, kv_width).astype(jnp.bfloat16),
            "ctx",
            scatter_dimension=0,
            tiled=True,
        ).astype(jnp.float32),
        lax.psum_scatter(
            value_grads.reshape(seq_rows, kv_width).astype(jnp.bfloat16),
            "ctx",
            scatter_dimension=0,
            tiled=True,
        ).astype(jnp.float32),
    )
    query_back, query_gain_grad = query_pull(query_grad.reshape(tok_rows, HEADS, HD))
    key_back, key_gain_grad = key_pull(key_sum.reshape(tok_rows, KV_HEADS, HD))
    proj_low = jnp.concatenate(
        [query_back.reshape(tok_rows, q_width), key_back.reshape(tok_rows, kv_width), value_sum],
        axis=1,
    ).astype(jnp.bfloat16)
    grad_qkv = jnp.einsum("ti,tj->ij", normed_low, proj_low, preferred_element_type=jnp.float32)
    normed_grad = jnp.einsum("tj,ij->ti", proj_low, full_qkv, preferred_element_type=jnp.float32)
    input_back, attn_gain_grad = attn_pull(normed_grad)
    input_grad = (hidden_grad + input_back).astype(jnp.bfloat16)
    grad_qkv, grad_out, grad_gate, grad_up, grad_down = (
        lax.psum_scatter(grad_qkv, ("ctx", "fsdp"), scatter_dimension=0, tiled=True),
        lax.psum_scatter(grad_out, ("ctx", "fsdp"), scatter_dimension=1, tiled=True),
        lax.psum_scatter(grad_gate, ("ctx", "fsdp"), scatter_dimension=0, tiled=True),
        lax.psum_scatter(grad_up, ("ctx", "fsdp"), scatter_dimension=0, tiled=True),
        lax.psum_scatter(grad_down, ("ctx", "fsdp"), scatter_dimension=1, tiled=True),
    )
    attn_gain_grad, ffn_gain_grad, query_gain_grad, key_gain_grad = lax.psum(
        (attn_gain_grad, ffn_gain_grad, query_gain_grad, key_gain_grad), ("ctx", "fsdp")
    )
    return (
        block_out.reshape(1, tok_rows, model_width),
        input_grad.reshape(1, tok_rows, model_width),
        grad_qkv,
        grad_out,
        grad_gate,
        grad_up,
        grad_down,
        attn_gain_grad,
        ffn_gain_grad,
        query_gain_grad,
        key_gain_grad,
    )


def solution(mesh):
    placed = (
        P("fsdp", "ctx", None),
        P("fsdp", "ctx", None),
        P("fsdp", None),
        P(("ctx", "fsdp"), None),
        P(None, ("ctx", "fsdp")),
        P(("ctx", "fsdp"), None),
        P(("ctx", "fsdp"), None),
        P(None, ("ctx", "fsdp")),
        P(),
        P(),
        P(),
        P(),
    )
    return jax.shard_map(
        body,
        mesh=mesh,
        in_specs=placed,
        out_specs=(
            P("fsdp", "ctx", None),
            P("fsdp", "ctx", None),
            P(("ctx", "fsdp"), None),
            P(None, ("ctx", "fsdp")),
            P(("ctx", "fsdp"), None),
            P(("ctx", "fsdp"), None),
            P(None, ("ctx", "fsdp")),
            P(),
            P(),
            P(),
            P(),
        ),
        check_vma=False,
    )
```

profile of v0, /device:TPU:0, one launch (start us, length us, event | category | flops | bytes accessed | tf_op | source)
XLA Modules:
  0.0 1676.6 jit_solution(10010941639250307840)
XLA Ops:
  12.1 63.5 %all-gather.8.cloned.1.call-done = bf16[1024,2048]{1,0:T(8,128)(2,1)} async-done(((bf16[32,2048]{1,0:T(8,128)(2,1)}), bf16[1024,2048]{1,0:T(8,128)(2,1)}) %all-gather.8.cloned.1.call-update) | async-done | bytes 4194320 | tf_op jit(solution)/shard_map/all_gather | solution.py:77
  91.7 40.6 %all-gather.12.cloned.1.call-done = bf16[2048,512]{1,0:T(8,128)(2,1)} async-done(((bf16[256,512]{1,0:T(8,128)(2,1)}), bf16[2048,512]{1,0:T(8,128)(2,1)}) %all-gather.12.cloned.1.call-update) | async-done | bytes 2097168 | tf_op jit(solution)/shard_map/all_gather | solution.py:99
  132.3 6.7 reshape.363
  144.5 38.3 %all-gather.10.cloned.1.call-done = bf16[2048,512]{1,0:T(8,128)(2,1)} async-done(((bf16[256,512]{1,0:T(8,128)(2,1)}), bf16[2048,512]{1,0:T(8,128)(2,1)}) %all-gather.10.cloned.1.call-update) | async-done | bytes 2097168 | tf_op jit(solution)/shard_map/all_gather | solution.py:100
  182.8 6.2 reshape.362
  194.4 45.0 %while.39 = (s32[]{:T(128)}, f32[8,2,256,1]{2,1,0,3:T(2,128)S(1)}, f32[8,2,256,1]{2,1,0,3:T(2,128)S(1)}, s32[256]{0:T(256)S(1)}, s32[4,512]{1,0:T(4,128)S(1)}, /...) while((s32[]{:T(128)}, f32[8,2,256,1]{2,1,0,3:T(2,128)S(1)}, ...), condition=%wide.region_7.8_spmd.clone, body=%wide.region_4.7_spmd.clone.sunk | while | flops 283267072 | bytes 18439788 | solution.py:117
  217.0 5.8 fusion.163
  239.5 21.2 %while.40 = (s32[]{:T(128)}, f32[256,8,2,64]{0,3,2,1:T(8,128)}, bf16[4,512,8,64]{1,3,2,0:T(8,128)(2,1)}, s32[256]{0:T(256)S(1)}, s32[4,512]{1,0:T(4,128)S(1)}, /...) while((s32[]{:T(128)}, f32[256,8,2,64]{0,3,2,1:T(8,128)}, ...), condition=%wide.region_9.10_spmd.clone, body=%wide.region_8.9_spmd.clone.sunk | while | flops 545914880 | bytes 3956851 | solution.py:135
  265.7 58.4 %all-gather.16.cloned.1.call-done = bf16[1024,4608]{1,0:T(8,128)(2,1)} async-done(((bf16[32,4608]{1,0:T(8,128)(2,1)}), bf16[1024,4608]{1,0:T(8,128)(2,1)}) %all-gather.16.cloned.1.call-update) | async-done | bytes 9437200 | tf_op jit(solution)/shard_map/all_gather | solution.py:79
  324.1 7.9 fusion.105
  332.0 75.5 %all-gather.18.cloned.1.call-done = bf16[1024,4608]{1,0:T(8,128)(2,1)} async-done(((bf16[32,4608]{1,0:T(8,128)(2,1)}), bf16[1024,4608]{1,0:T(8,128)(2,1)}) %all-gather.18.cloned.1.call-update) | async-done | bytes 9437200 | tf_op jit(solution)/shard_map/all_gather | solution.py:80
  407.5 8.1 fusion.106
  415.6 75.5 %all-gather.20.cloned.1.call-done = bf16[4608,1024]{0,1:T(8,128)(2,1)} async-done(((bf16[4608,32]{0,1:T(8,128)(2,1)}), bf16[4608,1024]{0,1:T(8,128)(2,1)}) %all-gather.20.cloned.1.call-update) | async-done | bytes 9437200 | tf_op jit(solution)/shard_map/all_gather | solution.py:81
  491.1 9.5 multiply_convert_fusion
  500.6 6.9 fusion.107
  517.7 89.8 %while.41 = (s32[]{:T(128)}, f32[256,8,2,64]{0,3,2,1:T(8,128)S(1)}, bf16[4,512,512]{2,1,0:T(8,128)(2,1)}, bf16[4,512,512]{2,1,0:T(8,128)(2,1)}, bf16[4,512,8,64]...) while((s32[]{:T(128)}, f32[256,8,2,64]{0,3,2,1:T(8,128)S(1)}, ...), condition=%wide.region_14.15_spmd.clone, body=%wide.region_13.14_spmd.clone.sunk | while | flops 1364590592 | bytes 101639392 | solution.py:206
  528.5 6.3 fusion.182
  550.8 6.3 fusion.182
  573.2 6.3 fusion.182
  595.7 6.3 fusion.182
  617.6 56.4 %reduce-scatter.8.cloned.1.call-done = bf16[256,512]{1,0:T(8,128)(2,1)} async-done(((bf16[2048,512]{1,0:T(8,128)(2,1)}), bf16[256,512]{1,0:T(8,128)(2,1)}) %reduce-scatter.8.cloned.1.call-update) | async-done | bytes 262160 | tf_op jit(solution)/shard_map/reduce_scatter | solution.py:210
  675.6 69.1 %reduce-scatter.10.cloned.1.call-done = bf16[256,512]{0,1:T(8,128)(2,1)} async-done(((bf16[2048,512]{0,1:T(8,128)(2,1)}), bf16[256,512]{0,1:T(8,128)(2,1)}) %reduce-scatter.10.cloned.1.call-update) | async-done | bytes 262160 | tf_op jit(solution)/shard_map/reduce_scatter | solution.py:216
  752.0 7.9 fusion.108
  761.6 8.2 fusion.109
  771.6 7.9 fusion.74
  780.7 8.0 fusion.59
  790.3 40.2 %all-reduce.4 = (f32[1024]{0:T(1024)}, f32[1024]{0:T(1024)}, f32[64]{0:T(128)}, f32[64]{0:T(128)}) all-reduce(f32[1024]{0:T(1024)S(1)} %get-tuple-element.334, f32[1024]{0:T(1024)S(1)} %get-tuple-element.332, f32[64]{0:T(128)S(1)} %get-tuple-element.336, f32[64]{0:T(128)S(1)} %get-tuple-element.338), channel_id=1, replica_groups=mesh['ctx'=8,'fsdp'=4] {'ctx','fsdp'}, use_global_device_ids=true, to_apply=%region_26.27 | all-reduce | flops 2176 | bytes 17408 | tf_op jit(solution)/shard_map/psum | solution.py:240
  831.6 55.6 %reduce-scatter.14.cloned.1.call-done = f32[1024,32]{0,1:T(8,128)} async-done(((f32[1024,1024]{0,1:T(8,128)}), f32[1024,32]{0,1:T(8,128)}) %reduce-scatter.14.cloned.1.call-update) | async-done | bytes 131088 | tf_op jit(solution)/shard_map/reduce_scatter | solution.py:235
  887.2 147.9 %reduce-scatter.12.cloned.1.call-done = f32[32,2048]{1,0:T(8,128)} async-done(((f32[1024,2048]{1,0:T(8,128)}), f32[32,2048]{1,0:T(8,128)}) %reduce-scatter.12.cloned.1.call-update) | async-done | bytes 262160 | tf_op jit(solution)/shard_map/reduce_scatter | solution.py:234
  1035.1 209.4 %reduce-scatter.16.cloned.1.call-done = f32[32,4608]{1,0:T(8,128)} async-done(((f32[1024,4608]{1,0:T(8,128)}), f32[32,4608]{1,0:T(8,128)}) %reduce-scatter.16.cloned.1.call-update) | async-done | bytes 589840 | tf_op jit(solution)/shard_map/reduce_scatter | solution.py:236
  1244.5 212.7 %reduce-scatter.18.cloned.1.call-done = f32[32,4608]{1,0:T(8,128)} async-done(((f32[1024,4608]{1,0:T(8,128)}), f32[32,4608]{1,0:T(8,128)}) %reduce-scatter.18.cloned.1.call-update) | async-done | bytes 589840 | tf_op jit(solution)/shard_map/reduce_scatter | solution.py:237
  1457.2 212.6 %reduce-scatter.20.cloned.1.call-done = f32[4608,32]{0,1:T(8,128)} async-done(((f32[4608,1024]{0,1:T(8,128)}), f32[4608,32]{0,1:T(8,128)}) %reduce-scatter.20.cloned.1.call-update) | async-done | bytes 589840 | tf_op jit(solution)/shard_map/reduce_scatter | solution.py:238
  (299 shorter events, 196.8 us)
Async XLA Ops:
  7.2 68.5 %all-gather.8.cloned.1.call-start = ((), (), s32[]{:S(2)}) async-start(), calls=%async_computation.7 | async-start | bytes 4325376 | tf_op jit(solution)/shard_map/all_gather | solution.py:77
  7.9 124.4 %all-gather.12.cloned.1.call-start = ((), (), s32[]{:S(2)}) async-start(), calls=%async_computation.9 | async-start | bytes 2359296 | tf_op jit(solution)/shard_map/all_gather | solution.py:99
  9.1 82.2 %copy-start.28 = (f32[256,64]{0,1:T(8,128)}, f32[256,64]{0,1:T(8,128)S(1)}, u32[]{:S(2)}) copy-start(f32[256,64]{0,1:T(8,128)S(1)} %get-tuple-element.417) | copy-start | bytes 196612
  9.1 82.2 %copy-start.30 = (f32[256,64]{0,1:T(8,128)}, f32[256,64]{0,1:T(8,128)S(1)}, u32[]{:S(2)}) copy-start(f32[256,64]{0,1:T(8,128)S(1)} %get-tuple-element.418) | copy-start | bytes 196612
  12.1 67.5 %copy-start.45 = (f32[256]{0:T(256)}, f32[256]{0:T(256)S(1)}, u32[]{:S(2)}) copy-start(f32[256]{0:T(256)S(1)} %fusion.66) | copy-start | bytes 3076
  12.1 67.5 %copy-start.43 = (f32[256]{0:T(256)}, f32[256]{0:T(256)S(1)}, u32[]{:S(2)}) copy-start(f32[256]{0:T(256)S(1)} %fusion.96) | copy-start | bytes 3076
  12.1 67.6 %copy-start.47 = (f32[64]{0:T(128)S(1)}, f32[64]{0:T(128)}, u32[]{:S(2)}) copy-start(f32[64]{0:T(128)} %param.29) | copy-start | bytes 772
  84.3 98.5 %all-gather.10.cloned.1.call-start = ((), (), s32[]{:S(2)}) async-start(), calls=%async_computation.8 | async-start | bytes 2359296 | tf_op jit(solution)/shard_map/all_gather | solution.py:100
  85.1 177.7 %all-gather.14.cloned.1.call-start = ((), (), s32[]{:S(2)}) async-start(), calls=%async_computation.10 | async-start | bytes 2162688 | tf_op jit(solution)/shard_map/all_gather | solution.py:78
  85.7 238.4 %all-gather.16.cloned.1.call-start = ((), (), s32[]{:S(2)}) async-start(), calls=%async_computation.11 | async-start | bytes 9732096 | tf_op jit(solution)/shard_map/all_gather | solution.py:79
  86.3 321.2 %all-gather.18.cloned.1.call-start = ((), (), s32[]{:S(2)}) async-start(), calls=%async_computation.12 | async-start | bytes 9732096 | tf_op jit(solution)/shard_map/all_gather | solution.py:80
  86.9 404.2 %all-gather.20.cloned.1.call-start = ((), (), s32[]{:S(2)}) async-start(), calls=%async_computation.13 | async-start | bytes 9732096 | tf_op jit(solution)/shard_map/all_gather | solution.py:81
  87.6 586.4 %reduce-scatter.8.cloned.1.call-start = ((), (), s32[]{:S(2)}) async-start(), calls=%async_computation.14 | async-start | bytes 2359296 | tf_op jit(solution)/shard_map/reduce_scatter | solution.py:210
  90.4 48.6 %copy-start.2 = (f32[256,1024]{0,1:T(8,128)}, f32[256,1024]{0,1:T(8,128)S(1)}, u32[]{:S(2)}) copy-start(f32[256,1024]{0,1:T(8,128)S(1)} %copy.75) | copy-start | bytes 3145732
  239.5 23.4 %copy-start.13 = (bf16[1,256,1024]{2,1,0:T(8,128)(2,1)S(1)}, bf16[1,256,1024]{2,1,0:T(8,128)(2,1)}, u32[]{:S(2)}) copy-start(bf16[1,256,1024]{2,1,0:T(8,128)(2,1)} %param.18) | copy-start | bytes 1572868
  265.5 246.1 %copy-start.10 = (f32[256,1024]{1,0:T(8,128)}, f32[256,1024]{1,0:T(8,128)S(1)}, u32[]{:S(2)}) copy-start(f32[256,1024]{1,0:T(8,128)S(1)} %get-tuple-element.420) | copy-start | bytes 3145732
  607.5 137.2 %reduce-scatter.10.cloned.1.call-start = ((), (), s32[]{:S(2)}) async-start(), calls=%async_computation.15 | async-start | bytes 2359296 | tf_op jit(solution)/shard_map/reduce_scatter | solution.py:216
  611.7 275.5 %reduce-scatter.14.cloned.1.call-start = ((), (), s32[]{:S(2)}) async-start(), calls=%async_computation.17 | async-start | bytes 4325376 | tf_op jit(solution)/shard_map/reduce_scatter | solution.py:235
  614.6 420.5 %reduce-scatter.12.cloned.1.call-start = ((), (), s32[]{:S(2)}) async-start(), calls=%async_computation.16 | async-start | bytes 8650752 | tf_op jit(solution)/shard_map/reduce_scatter | solution.py:234
  615.8 59.4 %copy-start.5 = (f32[256,512]{0,1:T(8,128)S(1)}, f32[256,512]{0,1:T(8,128)}, u32[]{:S(2)}) copy-start(f32[256,512]{0,1:T(8,128)} %copy-done.4) | copy-start | bytes 1572868
  615.8 59.4 %copy-start.36 = (f32[256,8]{0,1:T(8,128)S(1)}, f32[256,8]{0,1:T(8,128)}, u32[]{:S(2)}) copy-start(f32[256,8]{0,1:T(8,128)} %copy-done.35) | copy-start | bytes 24580
  615.8 59.4 %copy-start.48 = (f32[64]{0:T(128)S(1)}, f32[64]{0:T(128)}, u32[]{:S(2)}) copy-start(f32[64]{0:T(128)} %param.29) | copy-start | bytes 772
  616.4 59.0 %copy-start.41 = (f32[256,8]{0,1:T(8,128)S(1)}, f32[256,8]{0,1:T(8,128)}, u32[]{:S(2)}) copy-start(f32[256,8]{0,1:T(8,128)} %copy-done.40) | copy-start | bytes 24580
  616.5 128.2 %copy-start.14 = (bf16[1,256,1024]{2,1,0:T(8,128)(2,1)S(1)}, bf16[1,256,1024]{2,1,0:T(8,128)(2,1)}, u32[]{:S(2)}) copy-start(bf16[1,256,1024]{2,1,0:T(8,128)(2,1)} %param.18) | copy-start | bytes 1572868
  616.5 128.2 %copy-start.39 = (f32[1024]{0:T(1024)S(1)}, f32[1024]{0:T(1024)}, u32[]{:S(2)}) copy-start(f32[1024]{0:T(1024)} %param.26) | copy-start | bytes 12292
  616.5 128.2 %copy-start.44 = (f32[256]{0:T(256)S(1)}, f32[256]{0:T(256)}, u32[]{:S(2)}) copy-start(f32[256]{0:T(256)} %copy-done.43) | copy-start | bytes 3076
  617.6 127.1 %copy-start.24 = (bf16[256,16,64]{0,2,1:T(8,128)(2,1)S(1)}, bf16[256,16,64]{0,2,1:T(8,128)(2,1)}, u32[]{:S(2)}) copy-start(bf16[256,16,64]{0,2,1:T(8,128)(2,1)} %fusion.63) | copy-start | bytes 1572868
  750.4 494.1 %reduce-scatter.16.cloned.1.call-start = ((), (), s32[]{:S(2)}) async-start(), calls=%async_computation.18 | async-start | bytes 19464192 | tf_op jit(solution)/shard_map/reduce_scatter | solution.py:236
  759.9 697.3 %reduce-scatter.18.cloned.1.call-start = ((), (), s32[]{:S(2)}) async-start(), calls=%async_computation.19 | async-start | bytes 19464192 | tf_op jit(solution)/shard_map/reduce_scatter | solution.py:237
  769.8 899.9 %reduce-scatter.20.cloned.1.call-start = ((), (), s32[]{:S(2)}) async-start(), calls=%async_computation.20 | async-start | bytes 19464192 | tf_op jit(solution)/shard_map/reduce_scatter | solution.py:238
  788.7 41.8 %copy-start.46 = (f32[256]{0:T(256)S(1)}, f32[256]{0:T(256)}, u32[]{:S(2)}) copy-start(f32[256]{0:T(256)} %copy-done.45) | copy-start | bytes 3076
  788.7 41.8 %copy-start.8 = (f32[256,1024]{1,0:T(8,128)S(1)}, f32[256,1024]{1,0:T(8,128)}, u32[]{:S(2)}) copy-start(f32[256,1024]{1,0:T(8,128)} %copy-done.6) | copy-start | bytes 3145732
  (43 other events, 152.0 us)
Sparse Core Ops, SparseCore 0:
  10.9 64.7 all-gather.7
  84.4 47.8 all-gather.11
  135.0 47.7 all-gather.9
  185.5 54.8 all-gather.13
  243.2 80.8 all-gather.15
  326.8 80.6 all-gather.17
  410.4 80.6 all-gather.19
  607.6 66.2 reduce-scatter.7
  677.5 67.1 reduce-scatter.9
  747.4 139.7 reduce-scatter.13
  890.1 144.9 reduce-scatter.11
  1041.9 202.5 reduce-scatter.15
  1251.4 205.6 reduce-scatter.17
  1464.0 205.7 reduce-scatter.19
where the time goes:
time: 1680 us
  waiting for transfers between devices  1320 us (79%)
  matrix products  199 us (12%)
  local copies, waits for them, and re-layouts  66.2 us (4%)
  blocking collectives  40.2 us (2%)
  other arithmetic  35.7 us (2%)
    reduce_scatter x1, waiting for transfers between devices, body(): lax.psum_scatter(grad_up, ('ctx', 'fsdp'), scatter_dimension=0, tiled=True)  213 us
    reduce_scatter x1, waiting for transfers between devices, body(): lax.psum_scatter(grad_down, ('ctx', 'fsdp'), scatter_dimension=1, tiled=T...  213 us
    reduce_scatter x1, waiting for transfers between devices, body(): lax.psum_scatter(grad_gate, ('ctx', 'fsdp'), scatter_dimension=0, tiled=T...  209 us
    reduce_scatter x1, waiting for transfers between devices, body(): lax.psum_scatter(grad_qkv, ('ctx', 'fsdp'), scatter_dimension=0, tiled=True)  148 us
    all_gather x1, waiting for transfers between devices, body(): lax.all_gather(w_down, ('ctx', 'fsdp'), axis=1, tiled=True)  75.5 us
    all_gather x1, waiting for transfers between devices, body(): lax.all_gather(w_up, ('ctx', 'fsdp'), axis=0, tiled=True)  75.5 us
    reduce_scatter x1, waiting for transfers between devices, body(): lax.psum_scatter(value_grads.reshape(seq_rows, kv_width).astype(jnp.bfloa...  69.1 us
    all_gather x1, waiting for transfers between devices, body(): lax.all_gather(w_qkv, ('ctx', 'fsdp'), axis=0, tiled=True)  63.5 us
  transfers between devices with their start and end apart: 14, of which 13 were waited for; matrix products, arithmetic and copies ran while one was open for 10% of the time, Pallas kernels for 0%

commit v1 on v0

v1 whole, which is shorter than its diff:
```python
import jax
import jax.numpy as jnp
from jax import lax
from jax.experimental import pallas as pl
from jax.experimental.pallas import tpu as pltpu
from jax.sharding import PartitionSpec as P

HEADS = 16
KV_HEADS = 8
HD = 64
KBLOCK = 512


EPS = 1e-05
THETA = 1000000.0


def rms_norm(inputs, gain_row):
    return inputs * lax.rsqrt(jnp.mean(inputs * inputs, axis=-1, keepdims=True) + EPS) * gain_row


def rotary(inputs, cosines, sines):
    half_width = inputs.shape[-1] // 2
    turned = jnp.concatenate([-inputs[..., half_width:], inputs[..., :half_width]], axis=-1)
    return inputs * cosines + turned * sines


def angles(positions):
    exponent = jnp.arange(0, HD, 2).astype(jnp.float32) / HD
    inverse = jnp.power(THETA, -exponent)
    phases = positions.astype(jnp.float32)[:, None] * inverse[None, :]
    phases = jnp.concatenate([phases, phases], axis=-1)
    return (jnp.cos(phases)[:, None, :], jnp.sin(phases)[:, None, :])


PAIRS = KV_HEADS // 2
VMEM_LIMIT = 50 * 1024 * 1024


def forward_kernel(q_ref, kv_ref, qspot_ref, kspot_ref, out_ref, total_ref):
    query_cols = q_ref[0]
    query_spots = qspot_ref[...]

    def step(block, carry):
        mixed, total = carry
        rows = pl.ds(pl.multiple_of(block * KBLOCK, KBLOCK), KBLOCK)
        keys = kv_ref[rows, :128]
        values = kv_ref[rows, 128:]
        scores = jnp.dot(keys, query_cols, preferred_element_type=jnp.float32)
        allowed = query_spots >= kspot_ref[rows, :]
        weights = jnp.where(allowed, jnp.exp(scores), 0.0)
        total = total + jnp.sum(weights, axis=0, keepdims=True)
        mixed = mixed + lax.dot_general(
            values,
            weights.astype(jnp.bfloat16),
            (((0,), (0,)), ((), ())),
            preferred_element_type=jnp.float32,
        )
        return mixed, total

    columns = query_cols.shape[1]
    mixed, total = lax.fori_loop(
        0,
        kv_ref.shape[0] // KBLOCK,
        step,
        (jnp.zeros((128, columns), jnp.float32), jnp.zeros((1, columns), jnp.float32)),
    )
    out_ref[0] = mixed / total
    total_ref[0] = 1.0 / total


def backward_kernel(q_ref, do_ref, kv_ref, out_ref, inv_ref, qspot_ref, kspot_ref, dq_ref, dkv_ref):
    query_cols = q_ref[0]
    grad_cols = do_ref[0]
    query_spots = qspot_ref[...]
    inverse = inv_ref[0]
    diagonal = jnp.sum(grad_cols.astype(jnp.float32) * out_ref[0], axis=0, keepdims=True)
    last = (((1,), (1,)), ((), ()))

    def step(block, query_grad):
        rows = pl.ds(pl.multiple_of(block * KBLOCK, KBLOCK), KBLOCK)
        keys = kv_ref[rows, :128]
        values = kv_ref[rows, 128:]
        scores = jnp.dot(keys, query_cols, preferred_element_type=jnp.float32)
        allowed = query_spots >= kspot_ref[rows, :]
        probs = jnp.where(allowed, jnp.exp(scores), 0.0) * inverse
        prob_grad = jnp.dot(values, grad_cols, preferred_element_type=jnp.float32)
        score_low = (probs * (prob_grad - diagonal)).astype(jnp.bfloat16)
        dkv_ref[rows, :128] = lax.dot_general(
            score_low, query_cols, last, preferred_element_type=jnp.float32
        ).astype(jnp.bfloat16)
        dkv_ref[rows, 128:] = lax.dot_general(
            probs.astype(jnp.bfloat16), grad_cols, last, preferred_element_type=jnp.float32
        ).astype(jnp.bfloat16)
        return query_grad + lax.dot_general(
            keys, score_low, (((0,), (0,)), ((), ())), preferred_element_type=jnp.float32
        )

    dq_ref[0] = lax.fori_loop(
        0, kv_ref.shape[0] // KBLOCK, step, jnp.zeros(query_cols.shape, jnp.float32)
    )


def head_columns(rows_by_heads):
    tok_rows = rows_by_heads.shape[0]
    cols = rows_by_heads.reshape(tok_rows, PAIRS, 2, 2, HD).transpose(1, 4, 2, 3, 0)
    cols = cols.reshape(PAIRS, HD, 2, 2 * tok_rows)
    empty = jnp.zeros_like(cols[:, :, 0])
    top = jnp.concatenate([cols[:, :, 0], empty], axis=-1)
    low = jnp.concatenate([empty, cols[:, :, 1]], axis=-1)
    return jnp.concatenate([top, low], axis=1)


def column_heads(cols, tok_rows):
    top = cols[:, :HD, : 2 * tok_rows].reshape(PAIRS, HD, 2, tok_rows)
    low = cols[:, HD:, 2 * tok_rows :].reshape(PAIRS, HD, 2, tok_rows)
    both = jnp.stack([top, low], axis=1)
    return both.transpose(4, 0, 1, 3, 2).reshape(tok_rows, HEADS * HD)


def attend(query_cols, kv_all, query_row, key_col):
    seq_rows = kv_all.shape[0]
    columns = query_cols.shape[2]
    return pl.pallas_call(
        forward_kernel,
        grid=(PAIRS,),
        in_specs=[
            pl.BlockSpec((1, 128, columns), lambda p: (p, 0, 0)),
            pl.BlockSpec((seq_rows, 256), lambda p: (0, p)),
            pl.BlockSpec((1, columns), lambda p: (0, 0)),
            pl.BlockSpec((seq_rows, 1), lambda p: (0, 0)),
        ],
        out_specs=[
            pl.BlockSpec((1, 128, columns), lambda p: (p, 0, 0)),
            pl.BlockSpec((1, 1, columns), lambda p: (p, 0, 0)),
        ],
        out_shape=[
            jax.ShapeDtypeStruct((PAIRS, 128, columns), jnp.float32),
            jax.ShapeDtypeStruct((PAIRS, 1, columns), jnp.float32),
        ],
        compiler_params=pltpu.CompilerParams(vmem_limit_bytes=VMEM_LIMIT),
        cost_estimate=pl.CostEstimate(
            flops=4 * PAIRS * 128 * columns * seq_rows,
            bytes_accessed=12 * 1024 * 1024,
            transcendentals=PAIRS * columns * seq_rows,
        ),
    )(query_cols, kv_all, query_row, key_col)


def attend_back(query_cols, grad_cols, kv_all, mixed, inverse, query_row, key_col):
    seq_rows = kv_all.shape[0]
    columns = query_cols.shape[2]
    return pl.pallas_call(
        backward_kernel,
        grid=(PAIRS,),
        in_specs=[
            pl.BlockSpec((1, 128, columns), lambda p: (p, 0, 0)),
            pl.BlockSpec((1, 128, columns), lambda p: (p, 0, 0)),
            pl.BlockSpec((seq_rows, 256), lambda p: (0, p)),
            pl.BlockSpec((1, 128, columns), lambda p: (p, 0, 0)),
            pl.BlockSpec((1, 1, columns), lambda p: (p, 0, 0)),
            pl.BlockSpec((1, columns), lambda p: (0, 0)),
            pl.BlockSpec((seq_rows, 1), lambda p: (0, 0)),
        ],
        out_specs=[
            pl.BlockSpec((1, 128, columns), lambda p: (p, 0, 0)),
            pl.BlockSpec((seq_rows, 256), lambda p: (0, p)),
        ],
        out_shape=[
            jax.ShapeDtypeStruct((PAIRS, 128, columns), jnp.float32),
            jax.ShapeDtypeStruct((seq_rows, PAIRS * 256), jnp.bfloat16),
        ],
        compiler_params=pltpu.CompilerParams(vmem_limit_bytes=VMEM_LIMIT),
        cost_estimate=pl.CostEstimate(
            flops=10 * PAIRS * 128 * columns * seq_rows,
            bytes_accessed=20 * 1024 * 1024,
            transcendentals=PAIRS * columns * seq_rows,
        ),
    )(query_cols, grad_cols, kv_all, mixed, inverse, query_row, key_col)


def weave(left, right):
    tok_rows = left.shape[0]
    parts = [left.reshape(tok_rows, PAIRS, 128), right.reshape(tok_rows, PAIRS, 128)]
    return jnp.concatenate(parts, axis=-1).reshape(tok_rows, PAIRS * 256)


def unweave(both):
    tok_rows = both.shape[0]
    parts = both.reshape(tok_rows, PAIRS, 2, 128)
    return (
        parts[:, :, 0].reshape(tok_rows, PAIRS * 128),
        parts[:, :, 1].reshape(tok_rows, PAIRS * 128),
    )


def dot(left, right, left_dim, right_dim):
    return lax.dot_general(
        left, right, (((left_dim,), (right_dim,)), ((), ())), preferred_element_type=jnp.float32
    )


def body(
    tokens,
    cotangent,
    block_order,
    w_qkv,
    w_out,
    w_gate,
    w_up,
    w_down,
    attn_gain,
    ffn_gain,
    query_gain,
    key_gain,
):
    tok_rows = tokens.shape[1]
    model_width = tokens.shape[2]
    span_count = lax.axis_size("ctx")
    ways = lax.axis_size("fsdp")
    seq_rows = tok_rows * span_count
    half_rows = tok_rows // 2
    scale = HD ** (-0.5)
    q_width = HEADS * HD
    kv_width = KV_HEADS * HD
    own_rows = w_gate.shape[0]
    hidden_units = w_gate.shape[1]
    part = hidden_units // ways
    low = jnp.bfloat16
    slot_order = block_order.reshape(-1)
    key_spots = (
        slot_order[:, None] * half_rows + jnp.arange(half_rows, dtype=jnp.int32)[None, :]
    ).reshape(-1)
    query_spots = lax.dynamic_slice_in_dim(key_spots, lax.axis_index("ctx") * tok_rows, tok_rows)
    cosines, sines = angles(query_spots)
    key_col = key_spots[:, None]
    query_row = jnp.tile(query_spots, 4)[None, :]

    first_weights = lax.all_gather(
        jnp.concatenate([w_qkv, w_out.T], axis=1), ("ctx", "fsdp"), axis=0, tiled=True
    )
    full_qkv = first_weights[:, : w_qkv.shape[1]]
    out_t = first_weights[:, w_qkv.shape[1] :]
    ffn_own = jnp.concatenate(
        [
            w_gate.reshape(own_rows, ways, part),
            w_up.reshape(own_rows, ways, part),
            w_down.T.reshape(own_rows, ways, part),
        ],
        axis=-1,
    ).transpose(1, 0, 2)
    ffn_rows = lax.all_to_all(ffn_own, "fsdp", 0, 0, tiled=True)
    ffn_weights = lax.all_gather(
        ffn_rows.reshape(ways * own_rows, 3 * part), "ctx", axis=0, tiled=True
    )
    gate_part = ffn_weights[:, :part]
    up_part = ffn_weights[:, part : 2 * part]
    down_part = ffn_weights[:, 2 * part :]
    cot_low = cotangent.reshape(tok_rows, model_width)

    tok_f32 = tokens.reshape(tok_rows, model_width).astype(jnp.float32)
    normed, attn_pull = jax.vjp(rms_norm, tok_f32, attn_gain)
    normed_low = normed.astype(low)
    projected = jnp.dot(normed_low, full_qkv, preferred_element_type=jnp.float32)
    query_raw = projected[:, :q_width].reshape(tok_rows, HEADS, HD)
    key_raw = projected[:, q_width : q_width + kv_width].reshape(tok_rows, KV_HEADS, HD)
    value_low = projected[:, q_width + kv_width :].astype(low)

    def head_path(raw_heads, gain_row):
        return rotary(rms_norm(raw_heads, gain_row), cosines, sines)

    query_rot, query_pull = jax.vjp(head_path, query_raw, query_gain)
    key_rot, key_pull = jax.vjp(head_path, key_raw, key_gain)
    key_low = key_rot.astype(low).reshape(tok_rows, kv_width)
    kv_all = lax.all_gather(weave(key_low, value_low), "ctx", axis=0, tiled=True)
    query_cols = head_columns((query_rot.astype(low) * low(scale)).reshape(tok_rows, q_width))
    mixed, inverse = attend(query_cols, kv_all, query_row, key_col)
    attended_low = column_heads(mixed.astype(low), tok_rows)
    hidden = tok_f32 + dot(attended_low, out_t, 1, 1)
    normed_two, ffn_pull = jax.vjp(rms_norm, hidden, ffn_gain)
    cot_all = lax.all_gather(cot_low, "fsdp", axis=0, tiled=True)
    two_all = lax.all_gather(normed_two.astype(low), "fsdp", axis=0, tiled=True)

    gate_val = dot(two_all, gate_part, 1, 0)
    up_val = dot(two_all, up_part, 1, 0)

    def gated(gate_in, up_in):
        return jax.nn.silu(gate_in) * up_in

    activation, act_pull = jax.vjp(gated, gate_val, up_val)
    act_low = activation.astype(low)
    act_grad = dot(cot_all, down_part, 1, 0)
    gate_grad, up_grad = act_pull(act_grad)
    gate_low = gate_grad.astype(low)
    up_low = up_grad.astype(low)
    two_part = dot(gate_low, gate_part, 1, 1) + dot(up_low, up_part, 1, 1)
    normed_two_grad = lax.psum_scatter(
        two_part.astype(low), "fsdp", scatter_dimension=0, tiled=True
    ).astype(jnp.float32)
    block_part = dot(act_low, down_part, 1, 1)
    block_sum = lax.psum_scatter(
        block_part.astype(low), "fsdp", scatter_dimension=0, tiled=True
    ).astype(jnp.float32)
    block_out = (hidden + block_sum).astype(low)

    hidden_back, ffn_gain_grad = ffn_pull(normed_two_grad)
    hidden_grad = cot_low.astype(jnp.float32) + hidden_back
    hidden_low = hidden_grad.astype(low)
    attended_grad = dot(hidden_low, out_t, 1, 0).astype(low)
    grad_cols = head_columns(attended_grad)
    query_grad, kv_grad = attend_back(
        query_cols, grad_cols, kv_all, mixed, inverse, query_row, key_col
    )
    kv_sum = lax.psum_scatter(kv_grad, "ctx", scatter_dimension=0, tiled=True)
    key_sum, value_sum = unweave(kv_sum)

    grad_ffn = jnp.concatenate(
        [dot(two_all, gate_low, 0, 0), dot(two_all, up_low, 0, 0), dot(cot_all, act_low, 0, 0)],
        axis=1,
    ).astype(low)
    grad_ffn = lax.psum_scatter(grad_ffn, "ctx", scatter_dimension=0, tiled=True)
    grad_ffn = lax.all_to_all(
        grad_ffn.reshape(ways, own_rows, 3 * part), "fsdp", 0, 0, tiled=True
    ).transpose(1, 0, 2)
    grad_gate = grad_ffn[:, :, :part].reshape(own_rows, hidden_units).astype(jnp.float32)
    grad_up = grad_ffn[:, :, part : 2 * part].reshape(own_rows, hidden_units).astype(jnp.float32)
    grad_down = grad_ffn[:, :, 2 * part :].reshape(own_rows, hidden_units).T.astype(jnp.float32)

    query_back, query_gain_grad = query_pull(
        column_heads(query_grad * scale, tok_rows).reshape(tok_rows, HEADS, HD)
    )
    key_back, key_gain_grad = key_pull(
        key_sum.astype(jnp.float32).reshape(tok_rows, KV_HEADS, HD)
    )
    proj_low = jnp.concatenate(
        [
            query_back.reshape(tok_rows, q_width).astype(low),
            key_back.reshape(tok_rows, kv_width).astype(low),
            value_sum,
        ],
        axis=1,
    )
    grad_first = jnp.concatenate(
        [dot(normed_low, proj_low, 0, 0), dot(hidden_low, attended_low, 0, 0)], axis=1
    ).astype(low)
    grad_first = lax.psum_scatter(
        grad_first, ("ctx", "fsdp"), scatter_dimension=0, tiled=True
    ).astype(jnp.float32)
    grad_qkv = grad_first[:, : w_qkv.shape[1]]
    grad_out = grad_first[:, w_qkv.shape[1] :].T
    normed_grad = dot(proj_low, full_qkv, 1, 1)
    input_back, attn_gain_grad = attn_pull(normed_grad)
    input_grad = (hidden_grad + input_back).astype(low)
    attn_gain_grad, ffn_gain_grad, query_gain_grad, key_gain_grad = lax.psum(
        (attn_gain_grad, ffn_gain_grad, query_gain_grad, key_gain_grad), ("ctx", "fsdp")
    )
    return (
        block_out.reshape(1, tok_rows, model_width),
        input_grad.reshape(1, tok_rows, model_width),
        grad_qkv,
        grad_out,
        grad_gate,
        grad_up,
        grad_down,
        attn_gain_grad,
        ffn_gain_grad,
        query_gain_grad,
        key_gain_grad,
    )


def solution(mesh):
    placed = (
        P("fsdp", "ctx", None),
        P("fsdp", "ctx", None),
        P("fsdp", None),
        P(("ctx", "fsdp"), None),
        P(None, ("ctx", "fsdp")),
        P(("ctx", "fsdp"), None),
        P(("ctx", "fsdp"), None),
        P(None, ("ctx", "fsdp")),
        P(),
        P(),
        P(),
        P(),
    )
    return jax.shard_map(
        body,
        mesh=mesh,
        in_specs=placed,
        out_specs=(
            P("fsdp", "ctx", None),
            P("fsdp", "ctx", None),
            P(("ctx", "fsdp"), None),
            P(None, ("ctx", "fsdp")),
            P(("ctx", "fsdp"), None),
            P(("ctx", "fsdp"), None),
            P(None, ("ctx", "fsdp")),
            P(),
            P(),
            P(),
            P(),
        ),
        check_vma=False,
    )
```

time: 1680 us -> 805 us (0.48)
  waiting for transfers between devices: 1320 us -> 553 us
  matrix products: 199 us -> 62.5 us
  Pallas kernels: 0 us -> 42.3 us
  local copies, waits for them, and re-layouts: 66.2 us -> 37 us
    reduce_scatter x7 -> x5, waiting for transfers between devices: 964 us -> 311 us  [the longest x1 124 us: body(): lax.psum_scatter(grad_ffn, 'ctx', scatter_dimension=0, tiled=True)]
    dot_general x42 -> x14, matrix products: 196 us -> 58.8 us  [dot(): lax.dot_general(left, right, (((left_dim,), (right_dim,)), ((), ())), pre...]
    all_gather x7 -> x5, waiting for transfers between devices: 352 us -> 241 us  [the longest x1 103 us: body(): lax.all_gather(ffn_rows.reshape(ways * own_rows, 3 * part), 'ctx', axis=0...]
    pallas_call x0 -> x2, Pallas kernels: none -> 42.3 us  [the longest x1 26.6 us: attend_back(): pl.pallas_call(backward_kernel, grid=(PAIRS,), in_specs=[pl.BlockSpec((1,...]
    reduce_sum x6 -> x0, other arithmetic: 22.8 us -> none  [the longest x4 20.8 us: max_pass(): jnp.sum(jnp.exp(scores - new_top), axis=-1, keepdims=True)]
  transfers between devices with their start and end apart: 14 -> 11, of which waited for: 13 -> 9; matrix products, arithmetic and copies ran while one was open for 10% -> 9% of each run, Pallas kernels for 0% -> 2%
where the time goes in v1:
time: 805 us; the launch traced here: 797 us
  waiting for transfers between devices  553 us (69%)
  matrix products  62.5 us (8%)
  blocking collectives  56.1 us (7%)
  Pallas kernels  42.3 us (5%)
  local copies, waits for them, and re-layouts  37 us (5%)
  other arithmetic  26.8 us (3%)
  between operations  15.4 us (2%)
    reduce_scatter x1, waiting for transfers between devices, body(): lax.psum_scatter(grad_ffn, 'ctx', scatter_dimension=0, tiled=True)  124 us
    all_gather x1, waiting for transfers between devices, body(): lax.all_gather(ffn_rows.reshape(ways * own_rows, 3 * part), 'ctx', axis=0...  103 us
    all_gather x1, waiting for transfers between devices, body(): lax.all_gather(jnp.concatenate([w_qkv, w_out.T], axis=1), ('ctx', 'fsdp')...  71.7 us
    reduce_scatter x1, waiting for transfers between devices, body(): lax.psum_scatter(grad_first, ('ctx', 'fsdp'), scatter_dimension=0, tiled=...  65.3 us
    reduce_scatter x1, waiting for transfers between devices, body(): kv_sum = lax.psum_scatter(kv_grad, 'ctx', scatter_dimension=0, tiled=True)  64.4 us
    dot_general x14, matrix products, dot(): lax.dot_general(left, right, (((left_dim,), (right_dim,)), ((), ())), pre...  58.8 us
    all_gather x1, waiting for transfers between devices, body(): lax.all_gather(weave(key_low, value_low), 'ctx', axis=0, tiled=True)  51.2 us
    psum x1, blocking collectives, body(): lax.psum((attn_gain_grad, ffn_gain_grad, query_gain_grad, key_gain_grad),...  40.3 us
  transfers between devices with their start and end apart: 11, of which 9 were waited for; matrix products, arithmetic and copies ran while one was open for 9% of the time, Pallas kernels for 2%

profile of v1, /device:TPU:0, one launch (start us, length us, event | category | flops | bytes accessed | tf_op | source)
XLA Modules:
  0.0 797.4 jit_solution(17357920189446263232)
XLA Ops:
  11.9 71.7 %all-gather.7.cloned.1.call-done = bf16[1024,3072]{1,0:T(8,128)(2,1)} async-done(((bf16[32,3072]{1,0:T(8,128)(2,1)}), bf16[1024,3072]{1,0:T(8,128)(2,1)}) %all-gather.7.cloned.1.call-update) | async-done | bytes 6291472 | tf_op jit(solution)/shard_map/all_gather | solution.py:239
  83.7 3.7 fusion.7
  92.7 15.8 %all_to_all.10 = bf16[4,32,3456]{2,1,0:T(8,128)(2,1)} all-to-all(bf16[4,32,3456]{2,1,0:T(8,128)(2,1)S(1)} %copy.92), channel_id=1, replica_groups=mesh['ctx'=8,'fsdp'=4] {'fsdp'}, dimensions={0} | all-to-all | bytes 1769472 | tf_op jit(solution)/shard_map/all_to_all | solution.py:252
  112.0 51.2 %all-gather.9.cloned.1.call-done.kv_ref = bf16[2048,1024]{1,0:T(8,128)(2,1)} async-done(((bf16[256,1024]{1,0:T(8,128)(2,1)}), bf16[2048,1024]{1,0:T(8,128)(2,1)}) %all-gather.9.cloned.1.call-update) | async-done | bytes 4194320 | tf_op jit(solution)/shard_map/all_gather | solution.py:275
  163.2 15.6 %shard_map.203 = (f32[4,128,1024]{2,1,0:T(8,128)}, f32[4,1,1024]{2,1,0:T(1,128)S(1)}) custom-call(bf16[4,128,1024]{2,1,0:T(8,128)(2,1)S(1)} %fusion.56.q_ref, bf16[2048,1024]{1,0:T(8,128)(2,1)} %all-gather.9.cloned.1.call-done.kv_ref, s32[1,1024]{1,0:T(1,128)S(1)} %bitcast.142, s32[2048,1]{1,0:T(8,128)S(1)} %copy.89.kspot_ref), custom_call_target="tpu_custom_call" | custom-call | flops 4294967296 | bytes 12582912 | tf_op jit(solution)/shard_map/pallas_call | solution.py:124
  188.6 2.7 multiply_reduce_fusion.2
  193.6 102.9 %all-gather.13.cloned.1.call-done = bf16[1024,3456]{1,0:T(8,128)(2,1)} async-done(((bf16[128,3456]{1,0:T(8,128)(2,1)}), bf16[1024,3456]{1,0:T(8,128)(2,1)}) %all-gather.13.cloned.1.call-update) | async-done | bytes 7077904 | tf_op jit(solution)/shard_map/all_gather | solution.py:253
  296.5 7.3 fusion.15
  303.8 15.5 %all-gather.11.cloned.1.call-done = bf16[1024,1024]{1,0:T(8,128)(2,1)} async-done(((bf16[256,1024]{1,0:T(8,128)(2,1)}), bf16[1024,1024]{1,0:T(8,128)(2,1)}) %all-gather.11.cloned.1.call-update) | async-done | bytes 2097168 | tf_op jit(solution)/shard_map/all_gather | solution.py:282
  319.3 5.3 fusion.22
  325.6 7.1 fusion.2
  332.7 2.9 fusion.20
  335.6 4.2 add_convert_fusion
  339.9 6.6 fusion.28
  346.7 24.7 %reduce-scatter.8.cloned.1.call-done = bf16[256,1024]{1,0:T(8,128)(2,1)} async-done(((bf16[1024,1024]{1,0:T(8,128)(2,1)}), bf16[256,1024]{1,0:T(8,128)(2,1)}) %reduce-scatter.8.cloned.1.call-update) | async-done | bytes 524304 | tf_op jit(solution)/shard_map/reduce_scatter | solution.py:297
  373.2 32.4 %reduce-scatter.6.cloned.1.call-done = bf16[256,1024]{1,0:T(8,128)(2,1)} async-done(((bf16[1024,1024]{1,0:T(8,128)(2,1)}), bf16[256,1024]{1,0:T(8,128)(2,1)}) %reduce-scatter.6.cloned.1.call-update) | async-done | bytes 524304 | tf_op jit(solution)/shard_map/reduce_scatter | solution.py:301
  405.6 2.8 fusion.50
  409.4 3.1 fusion.39
  414.6 2.4 copy.95
  420.3 26.6 %shard_map.204 = (f32[4,128,1024]{2,1,0:T(8,128)}, bf16[2048,1024]{1,0:T(8,128)(2,1)}) custom-call(bf16[4,128,1024]{2,1,0:T(8,128)(2,1)S(1)} %fusion.56.q_ref, bf16[4,128,1024]{2,1,0:T(8,128)(2,1)S(1)} %fusion.57.do_ref, bf16[2048,1024]{1,0:T(8,128)(2,1)} %all-gather.9.cloned.1.call-done.kv_ref, f32[4,128,1024]{2,1,0:T(8,128)} %get-tuple-element.15.out_ref, ...), custom_call_target="tpu_custom_call" | custom-call | flops 10737418240 | bytes 20971520 | tf_op jit(solution)/shard_map/pallas_call | solution.py:153
  448.6 5.0 fusion.9
  453.6 3.2 convolution_convert_fusion.2
  456.8 3.2 convolution_convert_fusion.1
  460.0 3.4 pad_maximum_fusion
  470.7 64.4 %reduce-scatter.10.cloned.1.call-done = bf16[256,1024]{1,0:T(8,128)(2,1)} async-done(((bf16[2048,1024]{1,0:T(8,128)(2,1)}), bf16[256,1024]{1,0:T(8,128)(2,1)}) %reduce-scatter.10.cloned.1.call-update) | async-done | bytes 524304 | tf_op jit(solution)/shard_map/reduce_scatter | solution.py:314
  541.1 3.1 pad_maximum_fusion.1
  544.3 123.7 %reduce-scatter.14.cloned.1.call-done = bf16[128,3456]{1,0:T(8,128)(2,1)} async-done(((bf16[1024,3456]{1,0:T(8,128)(2,1)}), bf16[128,3456]{1,0:T(8,128)(2,1)}) %reduce-scatter.14.cloned.1.call-update) | async-done | bytes 884752 | tf_op jit(solution)/shard_map/reduce_scatter | solution.py:321
  668.1 3.5 all-to-all-start.1
  671.6 4.7 fusion.47
  676.3 40.3 %all-reduce.8 = (f32[1024]{0:T(1024)}, f32[1024]{0:T(1024)}, f32[64]{0:T(128)}, f32[64]{0:T(128)}) all-reduce(f32[1024]{0:T(1024)S(1)} %get-tuple-element.21, f32[1024]{0:T(1024)S(1)} %get-tuple-element.19, f32[64]{0:T(128)S(1)} %get-tuple-element.23, f32[64]{0:T(128)S(1)} %get-tuple-element.25), channel_id=1, replica_groups=mesh['ctx'=8,'fsdp'=4] {'ctx','fsdp'}, use_global_device_ids=true, to_apply=%region_14.15 | all-reduce | flops 2176 | bytes 17408 | tf_op jit(solution)/shard_map/psum | solution.py:354
  716.6 2.3 fusion.67
  721.6 65.3 %reduce-scatter.12.cloned.1.call-done = bf16[32,3072]{1,0:T(8,128)(2,1)} async-done(((bf16[1024,3072]{1,0:T(8,128)(2,1)}), bf16[32,3072]{1,0:T(8,128)(2,1)}) %reduce-scatter.12.cloned.1.call-update) | async-done | bytes 196624 | tf_op jit(solution)/shard_map/reduce_scatter | solution.py:346
  (180 shorter events, 55.1 us)
Async XLA Ops:
  7.2 76.5 %all-gather.7.cloned.1.call-start = ((), (), s32[]{:S(2)}) async-start(), calls=%async_computation.7 | async-start | bytes 6488064 | tf_op jit(solution)/shard_map/all_gather | solution.py:239
  8.9 154.3 %all-gather.9.cloned.1.call-start = ((), (), s32[]{:S(2)}) async-start(), calls=%async_computation.8 | async-start | bytes 4718592 | tf_op jit(solution)/shard_map/all_gather | solution.py:275
  87.4 1.8 copy-start.22
  89.9 2.0 copy-start.14
  90.0 2.0 copy-start.15
  90.1 2.1 copy-start.16
  91.1 102.5 %all-gather.15.cloned.1.call-start = ((), (), s32[]{:S(2)}) async-start(), calls=%async_computation.16 | async-start | bytes 2621440 | tf_op jit(solution)/shard_map/all_gather | solution.py:281
  91.9 204.6 %all-gather.13.cloned.1.call-start = ((), (), s32[]{:S(2)}) async-start(), calls=%async_computation.10 | async-start | bytes 7962624 | tf_op jit(solution)/shard_map/all_gather | solution.py:253
  108.5 210.8 %all-gather.11.cloned.1.call-start = ((), (), s32[]{:S(2)}) async-start(), calls=%async_computation.9 | async-start | bytes 2621440 | tf_op jit(solution)/shard_map/all_gather | solution.py:282
  188.6 2.8 copy-start.7
  188.6 3.8 copy-start.20
  193.4 178.1 %reduce-scatter.8.cloned.1.call-start = ((), (), s32[]{:S(2)}) async-start(), calls=%async_computation.12 | async-start | bytes 2621440 | tf_op jit(solution)/shard_map/reduce_scatter | solution.py:297
  319.3 5.3 copy-start.24
  319.3 5.3 copy-start.26
  319.3 6.3 copy-start.28
  332.7 2.9 copy-start.29
  332.7 2.9 copy-start.31
  339.8 65.8 %reduce-scatter.6.cloned.1.call-start = ((), (), s32[]{:S(2)}) async-start(), calls=%async_computation.11 | async-start | bytes 2621440 | tf_op jit(solution)/shard_map/reduce_scatter | solution.py:301
  346.5 188.6 %reduce-scatter.10.cloned.1.call-start = ((), (), s32[]{:S(2)}) async-start(), calls=%async_computation.13 | async-start | bytes 4718592 | tf_op jit(solution)/shard_map/reduce_scatter | solution.py:314
  447.0 221.0 %reduce-scatter.14.cloned.1.call-start = ((), (), s32[]{:S(2)}) async-start(), calls=%async_computation.15 | async-start | bytes 7962624 | tf_op jit(solution)/shard_map/reduce_scatter | solution.py:321
  448.6 5.0 copy-start.27
  448.6 5.0 copy-start.32
  453.6 3.2 copy-start.30
  463.5 1.6 copy-start.9
  463.5 323.4 %reduce-scatter.12.cloned.1.call-start = ((), (), s32[]{:S(2)}) async-start(), calls=%async_computation.14 | async-start | bytes 6488064 | tf_op jit(solution)/shard_map/reduce_scatter | solution.py:346
  536.5 1.9 copy-start.1
  538.8 2.2 copy-start.19
  539.6 1.6 copy-start.5
  544.3 127.3 %copy-start.11 = (bf16[1,256,1024]{2,1,0:T(8,128)(2,1)S(1)}, bf16[1,256,1024]{2,1,0:T(8,128)(2,1)}, u32[]{:S(2)}) copy-start(bf16[1,256,1024]{2,1,0:T(8,128)(2,1)} %param.12) | copy-start | bytes 1572868
  544.3 127.3 %copy-start.13 = (bf16[256,16,64]{0,2,1:T(8,128)(2,1)S(1)}, bf16[256,16,64]{0,2,1:T(8,128)(2,1)}, u32[]{:S(2)}) copy-start(bf16[256,16,64]{0,2,1:T(8,128)(2,1)} %fusion.51) | copy-start | bytes 1572868
  544.3 127.3 %copy-start.18 = (bf16[256,4,1,128]{0,3,1,2:T(8,128)(2,1)S(1)}, bf16[256,4,1,128]{0,3,1,2:T(8,128)(2,1)}, u32[]{:S(2)}) copy-start(bf16[256,4,1,128]{0,3,1,2:T(8,128)(2,1)} %copy-done.17) | copy-start | bytes 786436
  668.1 50.9 %all-to-all-start.1 = ((bf16[4,32,3456]{2,1,0:T(8,128)(2,1)}), bf16[4,32,3456]{2,1,0:T(8,128)(2,1)S(1)}, u32[]{:S(2)}, u32[]{:S(2)}) async-start(bf16[4,32,3456]{2,1,0:T(8,128)(2,1)} %bitcast.163), calls=%async_computation.6 | async-start | bytes 1769472 | tf_op jit(solution)/shard_map/all_to_all | solution.py:322
  (13 other events, 15.3 us)
Sparse Core Ops, SparseCore 0:
  11.4 72.1 all-gather.6
  91.3 71.8 all-gather.8
  164.8 20.8 all-gather.14
  187.7 108.7 all-gather.12
  298.5 20.7 all-gather.10
  340.0 31.4 reduce-scatter.7
  374.1 31.4 reduce-scatter.5
  447.1 87.9 reduce-scatter.9
  539.3 128.7 reduce-scatter.13
  673.5 113.3 reduce-scatter.11

commit v2 on v1

--- a/solution.py
+++ b/solution.py
@@ -1,3 +1,5 @@
+import functools
+
 import jax
 import jax.numpy as jnp
 from jax import lax
@@ -37,15 +39,21 @@
 VMEM_LIMIT = 50 * 1024 * 1024
 
 
+def key_depth(columns):
+    return KBLOCK if columns <= 1024 else KBLOCK // 2
+
+
 def forward_kernel(q_ref, kv_ref, qspot_ref, kspot_ref, out_ref, total_ref):
     query_cols = q_ref[0]
+    width, columns = query_cols.shape
+    depth = key_depth(columns)
     query_spots = qspot_ref[...]
 
     def step(block, carry):
         mixed, total = carry
-        rows = pl.ds(pl.multiple_of(block * KBLOCK, KBLOCK), KBLOCK)
-        keys = kv_ref[rows, :128]
-        values = kv_ref[rows, 128:]
+        rows = pl.ds(pl.multiple_of(block * depth, depth), depth)
+        keys = kv_ref[rows, :width]
+        values = kv_ref[rows, width:]
         scores = jnp.dot(keys, query_cols, preferred_element_type=jnp.float32)
         allowed = query_spots >= kspot_ref[rows, :]
         weights = jnp.where(allowed, jnp.exp(scores), 0.0)
@@ -58,12 +66,11 @@
         )
         return mixed, total
 
-    columns = query_cols.shape[1]
     mixed, total = lax.fori_loop(
         0,
-        kv_ref.shape[0] // KBLOCK,
+        kv_ref.shape[0] // depth,
         step,
-        (jnp.zeros((128, columns), jnp.float32), jnp.zeros((1, columns), jnp.float32)),
+        (jnp.zeros((width, columns), jnp.float32), jnp.zeros((1, columns), jnp.float32)),
     )
     out_ref[0] = mixed / total
     total_ref[0] = 1.0 / total
@@ -71,6 +78,8 @@
 
 def backward_kernel(q_ref, do_ref, kv_ref, out_ref, inv_ref, qspot_ref, kspot_ref, dq_ref, dkv_ref):
     query_cols = q_ref[0]
+    width, columns = query_cols.shape
+    depth = key_depth(columns)
     grad_cols = do_ref[0]
     query_spots = qspot_ref[...]
     inverse = inv_ref[0]
@@ -78,18 +87,18 @@
     last = (((1,), (1,)), ((), ()))
 
     def step(block, query_grad):
-        rows = pl.ds(pl.multiple_of(block * KBLOCK, KBLOCK), KBLOCK)
-        keys = kv_ref[rows, :128]
-        values = kv_ref[rows, 128:]
+        rows = pl.ds(pl.multiple_of(block * depth, depth), depth)
+        keys = kv_ref[rows, :width]
+        values = kv_ref[rows, width:]
         scores = jnp.dot(keys, query_cols, preferred_element_type=jnp.float32)
         allowed = query_spots >= kspot_ref[rows, :]
         probs = jnp.where(allowed, jnp.exp(scores), 0.0) * inverse
         prob_grad = jnp.dot(values, grad_cols, preferred_element_type=jnp.float32)
         score_low = (probs * (prob_grad - diagonal)).astype(jnp.bfloat16)
-        dkv_ref[rows, :128] = lax.dot_general(
+        dkv_ref[rows, :width] = lax.dot_general(
             score_low, query_cols, last, preferred_element_type=jnp.float32
         ).astype(jnp.bfloat16)
-        dkv_ref[rows, 128:] = lax.dot_general(
+        dkv_ref[rows, width:] = lax.dot_general(
             probs.astype(jnp.bfloat16), grad_cols, last, preferred_element_type=jnp.float32
         ).astype(jnp.bfloat16)
         return query_grad + lax.dot_general(
@@ -97,7 +106,7 @@
         )
 
     dq_ref[0] = lax.fori_loop(
-        0, kv_ref.shape[0] // KBLOCK, step, jnp.zeros(query_cols.shape, jnp.float32)
+        0, kv_ref.shape[0] // depth, step, jnp.zeros(query_cols.shape, jnp.float32)
     )
 
 
@@ -120,63 +129,124 @@
 
 def attend(query_cols, kv_all, query_row, key_col):
     seq_rows = kv_all.shape[0]
-    columns = query_cols.shape[2]
+    groups, width, columns = query_cols.shape
     return pl.pallas_call(
         forward_kernel,
-        grid=(PAIRS,),
+        grid=(groups,),
         in_specs=[
-            pl.BlockSpec((1, 128, columns), lambda p: (p, 0, 0)),
-            pl.BlockSpec((seq_rows, 256), lambda p: (0, p)),
+            pl.BlockSpec((1, width, columns), lambda p: (p, 0, 0)),
+            pl.BlockSpec((seq_rows, 2 * width), lambda p: (0, p)),
             pl.BlockSpec((1, columns), lambda p: (0, 0)),
             pl.BlockSpec((seq_rows, 1), lambda p: (0, 0)),
         ],
         out_specs=[
-            pl.BlockSpec((1, 128, columns), lambda p: (p, 0, 0)),
+            pl.BlockSpec((1, width, columns), lambda p: (p, 0, 0)),
             pl.BlockSpec((1, 1, columns), lambda p: (p, 0, 0)),
         ],
         out_shape=[
-            jax.ShapeDtypeStruct((PAIRS, 128, columns), jnp.float32),
-            jax.ShapeDtypeStruct((PAIRS, 1, columns), jnp.float32),
+            jax.ShapeDtypeStruct((groups, width, columns), jnp.float32),
+            jax.ShapeDtypeStruct((groups, 1, columns), jnp.float32),
         ],
         compiler_params=pltpu.CompilerParams(vmem_limit_bytes=VMEM_LIMIT),
         cost_estimate=pl.CostEstimate(
-            flops=4 * PAIRS * 128 * columns * seq_rows,
+            flops=4 * groups * width * columns * seq_rows,
             bytes_accessed=12 * 1024 * 1024,
-            transcendentals=PAIRS * columns * seq_rows,
+            transcendentals=groups * columns * seq_rows,
         ),
     )(query_cols, kv_all, query_row, key_col)
 
 
 def attend_back(query_cols, grad_cols, kv_all, mixed, inverse, query_row, key_col):
     seq_rows = kv_all.shape[0]
-    columns = query_cols.shape[2]
+    groups, width, columns = query_cols.shape
     return pl.pallas_call(
         backward_kernel,
-        grid=(PAIRS,),
+        grid=(groups,),
         in_specs=[
-            pl.BlockSpec((1, 128, columns), lambda p: (p, 0, 0)),
-            pl.BlockSpec((1, 128, columns), lambda p: (p, 0, 0)),
-            pl.BlockSpec((seq_rows, 256), lambda p: (0, p)),
-            pl.BlockSpec((1, 128, columns), lambda p: (p, 0, 0)),
+            pl.BlockSpec((1, width, columns), lambda p: (p, 0, 0)),
+            pl.BlockSpec((1, width, columns), lambda p: (p, 0, 0)),
+            pl.BlockSpec((seq_rows, 2 * width), lambda p: (0, p)),
+            pl.BlockSpec((1, width, columns), lambda p: (p, 0, 0)),
             pl.BlockSpec((1, 1, columns), lambda p: (p, 0, 0)),
             pl.BlockSpec((1, columns), lambda p: (0, 0)),
             pl.BlockSpec((seq_rows, 1), lambda p: (0, 0)),
         ],
         out_specs=[
-            pl.BlockSpec((1, 128, columns), lambda p: (p, 0, 0)),
-            pl.BlockSpec((seq_rows, 256), lambda p: (0, p)),
+            pl.BlockSpec((1, width, columns), lambda p: (p, 0, 0)),
+            pl.BlockSpec((seq_rows, 2 * width), lambda p: (0, p)),
         ],
         out_shape=[
-            jax.ShapeDtypeStruct((PAIRS, 128, columns), jnp.float32),
-            jax.ShapeDtypeStruct((seq_rows, PAIRS * 256), jnp.bfloat16),
+            jax.ShapeDtypeStruct((groups, width, columns), jnp.float32),
+            jax.ShapeDtypeStruct((seq_rows, groups * 2 * width), jnp.bfloat16),
         ],
         compiler_params=pltpu.CompilerParams(vmem_limit_bytes=VMEM_LIMIT),
         cost_estimate=pl.CostEstimate(
-            flops=10 * PAIRS * 128 * columns * seq_rows,
+            flops=10 * groups * width * columns * seq_rows,
             bytes_accessed=20 * 1024 * 1024,
-            transcendentals=PAIRS * columns * seq_rows,
+            transcendentals=groups * columns * seq_rows,
         ),
     )(query_cols, grad_cols, kv_all, mixed, inverse, query_row, key_col)
+
+
+def exchange_kernel(axis, count, spread, src, dst, own_sem, send_sems, recv_sems):
+    me = lax.axis_index(axis)
+    barrier = pltpu.get_barrier_semaphore()
+    for step in range(1, count):
+        pl.semaphore_signal(
+            barrier,
+            inc=1,
+            device_id={axis: lax.rem(me + step, count)},
+            device_id_type=pl.DeviceIdType.MESH,
+        )
+    pl.semaphore_wait(barrier, count - 1)
+    copies = []
+    for step in range(1, count):
+        peer = lax.rem(me + step, count)
+        copies.append(
+            pltpu.make_async_remote_copy(
+                src_ref=src if spread else src.at[peer],
+                dst_ref=dst.at[me],
+                send_sem=send_sems.at[step - 1],
+                recv_sem=recv_sems.at[step - 1],
+                device_id={axis: peer},
+                device_id_type=pl.DeviceIdType.MESH,
+            )
+        )
+    for copy in copies:
+        copy.start()
+    own = pltpu.make_async_copy(src if spread else src.at[me], dst.at[me], own_sem)
+    own.start()
+    own.wait()
+    for copy in copies:
+        copy.wait()
+
+
+def exchange(block, axis, number, spread=False):
+    count = lax.axis_size(axis)
+    shape = (count,) + (block.shape if spread else block.shape[1:])
+    return pl.pallas_call(
+        functools.partial(exchange_kernel, axis, count, spread),
+        in_specs=[pl.BlockSpec(memory_space=pl.ANY)],
+        out_specs=pl.BlockSpec(memory_space=pl.ANY),
+        out_shape=jax.ShapeDtypeStruct(shape, block.dtype),
+        scratch_shapes=[
+            pltpu.SemaphoreType.DMA,
+            pltpu.SemaphoreType.DMA((count - 1,)),
+            pltpu.SemaphoreType.DMA((count - 1,)),
+        ],
+        compiler_params=pltpu.CompilerParams(collective_id=number, has_side_effects=True),
+        cost_estimate=pl.CostEstimate(flops=0, bytes_accessed=40_000_000, transcendentals=0),
+    )(block)
+
+
+def split_heads(cols, spans):
+    total = cols.shape[1] // 2
+    return cols.reshape(HD, 2, total).transpose(2, 1, 0).reshape(spans, total // spans, 2 * HD)
+
+
+def join_heads(rows):
+    total = rows.shape[0]
+    return rows.reshape(total, 2, HD).transpose(2, 1, 0).reshape(1, HD, 2 * total)
 
 
 def weave(left, right):
@@ -249,18 +319,21 @@
         ],
         axis=-1,
     ).transpose(1, 0, 2)
-    ffn_rows = lax.all_to_all(ffn_own, "fsdp", 0, 0, tiled=True)
+    ffn_rows = exchange(ffn_own, "fsdp", 1)
+    cot_low = cotangent.reshape(tok_rows, model_width)
+    cot_all = exchange(cot_low, "fsdp", 2, spread=True).reshape(ways * tok_rows, model_width)
+    by_head = span_count == KV_HEADS
+
+    tok_f32 = tokens.reshape(tok_rows, model_width).astype(jnp.float32)
+    normed, attn_pull = jax.vjp(rms_norm, tok_f32, attn_gain)
+    normed_low = normed.astype(low)
+    normed_low, cot_all, ffn_rows = lax.optimization_barrier((normed_low, cot_all, ffn_rows))
     ffn_weights = lax.all_gather(
         ffn_rows.reshape(ways * own_rows, 3 * part), "ctx", axis=0, tiled=True
     )
     gate_part = ffn_weights[:, :part]
     up_part = ffn_weights[:, part : 2 * part]
     down_part = ffn_weights[:, 2 * part :]
-    cot_low = cotangent.reshape(tok_rows, model_width)
-
-    tok_f32 = tokens.reshape(tok_rows, model_width).astype(jnp.float32)
-    normed, attn_pull = jax.vjp(rms_norm, tok_f32, attn_gain)
-    normed_low = normed.astype(low)
     projected = jnp.dot(normed_low, full_qkv, preferred_element_type=jnp.float32)
     query_raw = projected[:, :q_width].reshape(tok_rows, HEADS, HD)
     key_raw = projected[:, q_width : q_width + kv_width].reshape(tok_rows, KV_HEADS, HD)
@@ -272,14 +345,33 @@
     query_rot, query_pull = jax.vjp(head_path, query_raw, query_gain)
     key_rot, key_pull = jax.vjp(head_path, key_raw, key_gain)
     key_low = key_rot.astype(low).reshape(tok_rows, kv_width)
-    kv_all = lax.all_gather(weave(key_low, value_low), "ctx", axis=0, tiled=True)
-    query_cols = head_columns((query_rot.astype(low) * low(scale)).reshape(tok_rows, q_width))
+    query_low = query_rot.astype(low) * low(scale)
+    if by_head:
+        query_row = jnp.tile(key_spots, 2)[None, :]
+        sent = jnp.concatenate(
+            [
+                query_low.reshape(tok_rows, KV_HEADS, 2 * HD),
+                key_low.reshape(tok_rows, KV_HEADS, HD),
+                value_low.reshape(tok_rows, KV_HEADS, HD),
+            ],
+            axis=-1,
+        ).transpose(1, 0, 2)
+        head_rows = exchange(sent, "ctx", 3).reshape(seq_rows, 4 * HD)
+        query_cols = join_heads(head_rows[:, : 2 * HD])
+        kv_all = head_rows[:, 2 * HD :]
+    else:
+        kv_all = lax.all_gather(weave(key_low, value_low), "ctx", axis=0, tiled=True)
+        query_cols = head_columns(query_low.reshape(tok_rows, q_width))
     mixed, inverse = attend(query_cols, kv_all, query_row, key_col)
-    attended_low = column_heads(mixed.astype(low), tok_rows)
+    if by_head:
+        attended_low = exchange(split_heads(mixed[0].astype(low), span_count), "ctx", 4)
+        attended_low = attended_low.transpose(1, 0, 2).reshape(tok_rows, q_width)
+    else:
+        attended_low = column_heads(mixed.astype(low), tok_rows)
     hidden = tok_f32 + dot(attended_low, out_t, 1, 1)
     normed_two, ffn_pull = jax.vjp(rms_norm, hidden, ffn_gain)
-    cot_all = lax.all_gather(cot_low, "fsdp", axis=0, tiled=True)
-    two_all = lax.all_gather(normed_two.astype(low), "fsdp", axis=0, tiled=True)
+    two_all = exchange(normed_two.astype(low), "fsdp", 5, spread=True)
+    two_all = two_all.reshape(ways * tok_rows, model_width)
 
     gate_val = dot(two_all, gate_part, 1, 0)
     up_val = dot(two_all, up_part, 1, 0)
@@ -293,32 +385,47 @@
     gate_grad, up_grad = act_pull(act_grad)
     gate_low = gate_grad.astype(low)
     up_low = up_grad.astype(low)
+    grad_ffn = jnp.concatenate(
+        [dot(two_all, gate_low, 0, 0), dot(two_all, up_low, 0, 0), dot(cot_all, act_low, 0, 0)],
+        axis=1,
+    ).astype(low)
+    gate_low, up_low, act_low, grad_ffn = lax.optimization_barrier(
+        (gate_low, up_low, act_low, grad_ffn)
+    )
+    grad_ffn = lax.psum_scatter(grad_ffn, "ctx", scatter_dimension=0, tiled=True)
     two_part = dot(gate_low, gate_part, 1, 1) + dot(up_low, up_part, 1, 1)
-    normed_two_grad = lax.psum_scatter(
-        two_part.astype(low), "fsdp", scatter_dimension=0, tiled=True
-    ).astype(jnp.float32)
-    block_part = dot(act_low, down_part, 1, 1)
-    block_sum = lax.psum_scatter(
-        block_part.astype(low), "fsdp", scatter_dimension=0, tiled=True
-    ).astype(jnp.float32)
-    block_out = (hidden + block_sum).astype(low)
+    two_parts = two_part.astype(low).reshape(ways, tok_rows, model_width)
+    normed_two_grad = jnp.sum(exchange(two_parts, "fsdp", 6).astype(jnp.float32), axis=0)
 
     hidden_back, ffn_gain_grad = ffn_pull(normed_two_grad)
     hidden_grad = cot_low.astype(jnp.float32) + hidden_back
     hidden_low = hidden_grad.astype(low)
     attended_grad = dot(hidden_low, out_t, 1, 0).astype(low)
-    grad_cols = head_columns(attended_grad)
+    if by_head:
+        grad_rows = attended_grad.reshape(tok_rows, KV_HEADS, 2 * HD).transpose(1, 0, 2)
+        grad_cols = join_heads(exchange(grad_rows, "ctx", 7).reshape(seq_rows, 2 * HD))
+    else:
+        grad_cols = head_columns(attended_grad)
     query_grad, kv_grad = attend_back(
         query_cols, grad_cols, kv_all, mixed, inverse, query_row, key_col
     )
-    kv_sum = lax.psum_scatter(kv_grad, "ctx", scatter_dimension=0, tiled=True)
-    key_sum, value_sum = unweave(kv_sum)
-
-    grad_ffn = jnp.concatenate(
-        [dot(two_all, gate_low, 0, 0), dot(two_all, up_low, 0, 0), dot(cot_all, act_low, 0, 0)],
-        axis=1,
-    ).astype(low)
-    grad_ffn = lax.psum_scatter(grad_ffn, "ctx", scatter_dimension=0, tiled=True)
+    if by_head:
+        sent = jnp.concatenate(
+            [
+                split_heads((query_grad[0] * scale).astype(low), span_count),
+                kv_grad.reshape(span_count, tok_rows, 2 * HD),
+            ],
+            axis=-1,
+        )
+        received = exchange(sent, "ctx", 8).transpose(1, 0, 2)
+        query_sum = received[:, :, : 2 * HD].astype(jnp.float32)
+        key_sum = received[:, :, 2 * HD : 3 * HD]
+        value_sum = received[:, :, 3 * HD :].reshape(tok_rows, kv_width)
+    else:
+        query_sum = column_heads(query_grad * scale, tok_rows)
+        kv_sum = lax.psum_scatter(kv_grad, "ctx", scatter_dimension=0, tiled=True)
+        key_sum, value_sum = unweave(kv_sum)
+
     grad_ffn = lax.all_to_all(
         grad_ffn.reshape(ways, own_rows, 3 * part), "fsdp", 0, 0, tiled=True
     ).transpose(1, 0, 2)
@@ -327,7 +434,7 @@
     grad_down = grad_ffn[:, :, 2 * part :].reshape(own_rows, hidden_units).T.astype(jnp.float32)
 
     query_back, query_gain_grad = query_pull(
-        column_heads(query_grad * scale, tok_rows).reshape(tok_rows, HEADS, HD)
+        query_sum.reshape(tok_rows, HEADS, HD)
     )
     key_back, key_gain_grad = key_pull(
         key_sum.astype(jnp.float32).reshape(tok_rows, KV_HEADS, HD)
@@ -343,6 +450,10 @@
     grad_first = jnp.concatenate(
         [dot(normed_low, proj_low, 0, 0), dot(hidden_low, attended_low, 0, 0)], axis=1
     ).astype(low)
+    grad_first, act_low = lax.optimization_barrier((grad_first, act_low))
+    block_parts = dot(act_low, down_part, 1, 1).astype(low).reshape(ways, tok_rows, model_width)
+    block_sum = jnp.sum(exchange(block_parts, "fsdp", 9).astype(jnp.float32), axis=0)
+    block_out = (hidden + block_sum).astype(low)
     grad_first = lax.psum_scatter(
         grad_first, ("ctx", "fsdp"), scatter_dimension=0, tiled=True
     ).astype(jnp.float32)

time: 805 us -> 574 us (0.71)
  waiting for transfers between devices: 553 us -> 60.6 us
  Pallas kernels: 42.3 us -> 291 us
  local copies, waits for them, and re-layouts: 37 us -> 46.6 us
    pallas_call x2 -> x11, Pallas kernels: 42.3 us -> 291 us  [the longest x9 253 us: exchange(): pl.pallas_call(functools.partial(exchange_kernel, axis, count, spread), i...]
    reduce_scatter x1, waiting for transfers between devices: 124 us -> 0.01 us  [body(): lax.psum_scatter(grad_ffn, 'ctx', scatter_dimension=0, tiled=True)]
    reduce_scatter x3 -> x0, waiting for transfers between devices: 122 us -> none  [the longest x1 64.4 us: body(): kv_sum = lax.psum_scatter(kv_grad, 'ctx', scatter_dimension=0, tiled=True)]
    all_gather x1, waiting for transfers between devices: 103 us -> 4.19 us  [body(): lax.all_gather(ffn_rows.reshape(ways * own_rows, 3 * part), 'ctx', axis=0...]
    all_gather x3 -> x0, waiting for transfers between devices: 66.7 us -> none  [the longest x1 51.2 us: body(): lax.all_gather(weave(key_low, value_low), 'ctx', axis=0, tiled=True)]
    all_gather x1, waiting for transfers between devices: 71.7 us -> 26.8 us  [body(): lax.all_gather(jnp.concatenate([w_qkv, w_out.T], axis=1), ('ctx', 'fsdp')...]
    reduce_scatter x1, waiting for transfers between devices: 65.3 us -> 29.5 us  [body(): lax.psum_scatter(grad_first, ('ctx', 'fsdp'), scatter_dimension=0, tiled=...]
    all_to_all x1 -> x0, blocking collectives: 15.8 us -> none  [body(): ffn_rows = lax.all_to_all(ffn_own, 'fsdp', 0, 0, tiled=True)]
  transfers between devices with their start and end apart: 11 -> 5, of which waited for: 9 -> 3; matrix products, arithmetic and copies ran while one was open for 9% -> 18% of each run, Pallas kernels for 2% -> 51%
where the time goes in v2:
time: 574 us; the launch traced here: 566 us
  Pallas kernels  291 us (51%)
  matrix products  60.7 us (11%)
  waiting for transfers between devices  60.6 us (11%)
  blocking collectives  54.3 us (9%)
  local copies, waits for them, and re-layouts  46.6 us (8%)
  other arithmetic  34.2 us (6%)
  between operations  15 us (3%)
    pallas_call x9, Pallas kernels, exchange(): pl.pallas_call(functools.partial(exchange_kernel, axis, count, spread), i...  253 us
    dot_general x14, matrix products, dot(): lax.dot_general(left, right, (((left_dim,), (right_dim,)), ((), ())), pre...  57.3 us
    psum x1, blocking collectives, body(): lax.psum((attn_gain_grad, ffn_gain_grad, query_gain_grad, key_gain_grad),...  54.3 us
    reduce_scatter x1, waiting for transfers between devices, body(): lax.psum_scatter(grad_first, ('ctx', 'fsdp'), scatter_dimension=0, tiled=...  29.5 us
    all_gather x1, waiting for transfers between devices, body(): lax.all_gather(jnp.concatenate([w_qkv, w_out.T], axis=1), ('ctx', 'fsdp')...  26.8 us
    pallas_call x1, Pallas kernels, attend_back(): pl.pallas_call(backward_kernel, grid=(groups,), in_specs=[pl.BlockSpec((1...  25.2 us
    pallas_call x1, Pallas kernels, attend(): pl.pallas_call(forward_kernel, grid=(groups,), in_specs=[pl.BlockSpec((1,...  12 us
  transfers between devices with their start and end apart: 5, of which 3 were waited for; matrix products, arithmetic and copies ran while one was open for 18% of the time, Pallas kernels for 51%

profile of v2, /device:TPU:0, one launch (start us, length us, event | category | flops | bytes accessed | tf_op | source)
XLA Modules:
  0.0 565.6 jit_solution(15123167190127066435)
XLA Ops:
  12.0 14.7 %shard_map.204 = bf16[4,32,3456]{2,1,0:T(8,128)(2,1)} custom-call(bf16[4,32,3456]{2,1,0:T(8,128)(2,1)} %maximum_bitcast_fusion.1.src), custom_call_target="tpu_custom_call" | custom-call | bytes 40000000 | tf_op jit(solution)/shard_map/pallas_call | solution.py:227
  26.8 31.2 %shard_map.203 = bf16[4,256,1024]{2,1,0:T(8,128)(2,1)} custom-call(bf16[256,1024]{1,0:T(8,128)(2,1)} %bitcast.144), custom_call_target="tpu_custom_call" | custom-call | bytes 40000000 | tf_op jit(solution)/shard_map/pallas_call | solution.py:227
  62.7 26.8 %all-gather.3.cloned.1.call-done = bf16[1024,3072]{1,0:T(8,128)(2,1)} async-done(((bf16[32,3072]{1,0:T(8,128)(2,1)}), bf16[1024,3072]{1,0:T(8,128)(2,1)}) %all-gather.3.cloned.1.call-update) | async-done | bytes 6291472 | tf_op jit(solution)/shard_map/all_gather | solution.py:309
  89.5 3.4 fusion.6
  101.3 2.5 copy.41
  105.0 2.5 copy.37
  115.0 30.3 %shard_map.205 = bf16[8,256,256]{2,1,0:T(8,128)(2,1)} custom-call(bf16[8,256,256]{2,1,0:T(8,128)(2,1)} %maximum_bitcast_fusion.src), custom_call_target="tpu_custom_call" | custom-call | bytes 40000000 | tf_op jit(solution)/shard_map/pallas_call | solution.py:227
  147.8 12.0 %shard_map.206 = (f32[1,64,4096]{2,1,0:T(8,128)S(1)}, f32[1,1,4096]{2,1,0:T(1,128)S(1)}) custom-call(bf16[1,64,4096]{2,1,0:T(8,128)(2,1)S(1)} %reshape.336.q_ref, bf16[2048,128]{1,0:T(8,128)(2,1)S(1)} %get-tuple-element.58.kv_ref, s32[1,4096]{1,0:T(1,128)S(1)} %bitcast.117, s32[2048,1]{1,0:T(8,128)S(1)} %copy.48.kspot_ref), custom_call_target="tpu_custom_call" | custom-call | flops 2147483648 | bytes 12582912 | tf_op jit(solution)/shard_map/pallas_call | solution.py:133
  162.0 28.8 %shard_map.207 = bf16[8,256,128]{2,1,0:T(8,128)(2,1)} custom-call(bf16[8,256,128]{2,1,0:T(8,128)(2,1)} %copy.50.src), custom_call_target="tpu_custom_call" | custom-call | bytes 40000000 | tf_op jit(solution)/shard_map/pallas_call | solution.py:227
  192.1 2.7 multiply_reduce_fusion.6
  195.8 24.8 %shard_map.208 = bf16[4,256,1024]{2,1,0:T(8,128)(2,1)} custom-call(bf16[256,1024]{1,0:T(8,128)(2,1)} %multiply_convert_fusion.3.src), custom_call_target="tpu_custom_call" | custom-call | bytes 40000000 | tf_op jit(solution)/shard_map/pallas_call | solution.py:227
  220.6 4.2 all-gather.5.cloned.1.call-done
  224.8 5.3 fusion.10
  230.2 2.9 fusion.18
  233.1 6.9 %multiply_convert_fusion = (bf16[1024,1152]{1,0:T(8,128)(2,1)}, bf16[1024,1152]{1,0:T(8,128)(2,1)S(1)}, bf16[1024,1152]{1,0:T(8,128)(2,1)}) fusion(f32[1024,1152]{1,0:T(8,128)S(1)} %fusion.10, f32[1024,1152]{1,0:T(8,128)S(1)} %fusion.18, bf16[1024,1024]{1,0:T(8,128)(2,1)S(1)} %bitcast.137, bf16[1024,3456]{1,0:T(8,128)(2,1)S(1)} %copy-done.41), kind=kOutput, calls=%fused_computation.6 | convolution fusion | flops 2434793472 | bytes 20971520 | tf_op jit(solution)/shard_map/dot_general | solution.py:268
  240.0 5.7 %convolution_convert_fusion.1 = bf16[1024,1152]{1,0:T(8,128)(2,1)S(1)} fusion(bf16[1024,1024]{1,0:T(8,128)(2,1)S(1)} %bitcast.135, bf16[1024,1152]{1,0:T(8,128)(2,1)} %get-tuple-element.34), kind=kOutput, calls=%fused_computation.14 | convolution fusion | flops 2417098752 | bytes 6815744 | tf_op jit(solution)/shard_map/dot_general | solution.py:268
  245.7 3.2 convolution_convert_fusion.3
  248.9 3.2 convolution_convert_fusion.2
  252.1 3.4 pad_maximum_fusion
  255.6 5.4 fusion.8
  261.1 6.0 %add_convert_fusion = bf16[1024,1024]{1,0:T(8,128)(2,1)} fusion(f32[1024,1024]{1,0:T(8,128)S(1)} %fusion.8, bf16[1024,1152]{1,0:T(8,128)(2,1)S(1)} %copy-done.45, bf16[1024,3456]{1,0:T(8,128)(2,1)} %all-gather.5.cloned.1.call-done), kind=kOutput, calls=%fused_computation.12 | convolution fusion | flops 2418016256 | bytes 11010048 | tf_op jit(solution)/shard_map/dot_general | solution.py:268
  267.1 24.9 %shard_map.209 = bf16[4,256,1024]{2,1,0:T(8,128)(2,1)} custom-call(bf16[4,256,1024]{2,1,0:T(8,128)(2,1)} %bitcast.142), custom_call_target="tpu_custom_call" | custom-call | bytes 40000000 | tf_op jit(solution)/shard_map/pallas_call | solution.py:227
  300.0 27.9 %shard_map.210 = bf16[8,256,128]{2,1,0:T(8,128)(2,1)} custom-call(bf16[8,256,128]{2,1,0:T(8,128)(2,1)} %bitcast.150), custom_call_target="tpu_custom_call" | custom-call | bytes 40000000 | tf_op jit(solution)/shard_map/pallas_call | solution.py:227
  330.6 25.2 %shard_map.211 = (f32[1,64,4096]{2,1,0:T(8,128)S(1)}, bf16[2048,128]{1,0:T(8,128)(2,1)S(1)}) custom-call(bf16[1,64,4096]{2,1,0:T(8,128)(2,1)S(1)} %reshape.336.q_ref, bf16[1,64,4096]{2,1,0:T(8,128)(2,1)S(1)} %reshape.343.do_ref, bf16[2048,128]{1,0:T(8,128)(2,1)S(1)} %get-tuple-element.58.kv_ref, f32[1,64,4096]{2,1,0:T(8,128)} %copy-done, ...), custom_call_target="tpu_custom_call" | custom-call | flops 5368709120 | bytes 20971520 | tf_op jit(solution)/shard_map/pallas_call | solution.py:162
  358.1 46.8 %shard_map.212 = bf16[8,256,256]{2,1,0:T(8,128)(2,1)} custom-call(bf16[8,256,256]{2,1,0:T(8,128)(2,1)} %pad_maximum_fusion.2.src), custom_call_target="tpu_custom_call" | custom-call | bytes 40000000 | tf_op jit(solution)/shard_map/pallas_call | solution.py:227
  421.6 3.2 pad_maximum_fusion.1
  424.8 6.6 %fusion.20 = bf16[1024,1024]{1,0:T(8,128)(2,1)} fusion(bf16[1024,1152]{1,0:T(8,128)(2,1)} %get-tuple-element.34, bf16[1024,3456]{1,0:T(8,128)(2,1)} %all-gather.5.cloned.1.call-done), kind=kOutput, calls=%fused_computation.38 | convolution fusion | flops 2416967680 | bytes 6815744 | tf_op jit(solution)/shard_map/dot_general | solution.py:268
  431.5 23.8 %shard_map.213 = bf16[4,256,1024]{2,1,0:T(8,128)(2,1)} custom-call(bf16[4,256,1024]{2,1,0:T(8,128)(2,1)} %bitcast.143), custom_call_target="tpu_custom_call" | custom-call | bytes 40000000 | tf_op jit(solution)/shard_map/pallas_call | solution.py:227
  455.3 4.8 fusion.37
  460.1 54.3 %all-reduce.4 = (f32[1024]{0:T(1024)}, f32[1024]{0:T(1024)}, f32[64]{0:T(128)}, f32[64]{0:T(128)}) all-reduce(f32[1024]{0:T(1024)S(1)} %get-tuple-element.41, f32[1024]{0:T(1024)S(1)} %copy-done.32, f32[64]{0:T(128)S(1)} %get-tuple-element.43, f32[64]{0:T(128)S(1)} %get-tuple-element.37), channel_id=1, replica_groups=mesh['ctx'=8,'fsdp'=4] {'ctx','fsdp'}, use_global_device_ids=true, to_apply=%region_13.14 | all-reduce | flops 2176 | bytes 17408 | tf_op jit(solution)/shard_map/psum | solution.py:465
  517.5 3.5 all-to-all-start
  523.4 29.5 %reduce-scatter.3.cloned.1.call-done = bf16[32,3072]{1,0:T(8,128)(2,1)} async-done(((bf16[1024,3072]{1,0:T(8,128)(2,1)}), bf16[32,3072]{1,0:T(8,128)(2,1)}) %reduce-scatter.3.cloned.1.call-update) | async-done | bytes 196624 | tf_op jit(solution)/shard_map/reduce_scatter | solution.py:457
  (203 shorter events, 73.9 us)
Async XLA Ops:
  7.2 82.3 %all-gather.3.cloned.1.call-start = ((), (), s32[]{:S(2)}) async-start(), calls=%async_computation.3 | async-start | bytes 6488064 | tf_op jit(solution)/shard_map/all_gather | solution.py:309
  8.9 215.9 %all-gather.5.cloned.1.call-start = ((), (), s32[]{:S(2)}) async-start(), calls=%async_computation.4 | async-start | bytes 7962624 | tf_op jit(solution)/shard_map/all_gather | solution.py:331
  12.0 46.0 %copy-start.9 = (bf16[1,256,1024]{2,1,0:T(8,128)(2,1)S(1)}, bf16[1,256,1024]{2,1,0:T(8,128)(2,1)}, u32[]{:S(2)}) copy-start(bf16[1,256,1024]{2,1,0:T(8,128)(2,1)} %param.12) | copy-start | bytes 1572868
  12.0 46.8 %copy-start.30 = (f32[1024]{0:T(1024)S(1)}, f32[1024]{0:T(1024)}, u32[]{:S(2)}) copy-start(f32[1024]{0:T(1024)} %param.20) | copy-start | bytes 12292
  26.8 32.3 %copy-start.39 = (f32[64]{0:T(128)S(1)}, f32[64]{0:T(128)}, u32[]{:S(2)}) copy-start(f32[64]{0:T(128)} %param.22) | copy-start | bytes 772
  26.8 32.4 %copy-start.42 = (s32[1,16]{1,0:T(1,128)S(1)}, s32[1,16]{1,0:T(1,128)}, u32[]{:S(2)}) copy-start(s32[1,16]{1,0:T(1,128)} %param.14) | copy-start | bytes 196
  59.0 30.5 %copy-start.15 = (bf16[256,1024]{1,0:T(8,128)(2,1)}, bf16[256,1024]{1,0:T(8,128)(2,1)S(1)}, u32[]{:S(2)}) copy-start(bf16[256,1024]{1,0:T(8,128)(2,1)S(1)} %fusion.36) | copy-start | bytes 1572868
  59.0 458.4 %reduce-scatter.5.cloned.1.call-start = ((), (), s32[]{:S(2)}) async-start(), calls=%async_computation.6 | async-start | bytes 7962624 | tf_op jit(solution)/shard_map/reduce_scatter | solution.py:395
  61.2 86.5 %copy-start.1 = (s32[2048,1]{1,0:T(8,128)}, s32[2048,1]{1,0:T(8,128)S(1)}, u32[]{:S(2)}) copy-start(s32[2048,1]{1,0:T(8,128)S(1)} %copy.48.kspot_ref) | copy-start | bytes 24580
  95.3 12.1 %copy-start.2 = (f32[256,1024]{0,1:T(8,128)}, f32[256,1024]{0,1:T(8,128)S(1)}, u32[]{:S(2)}) copy-start(f32[256,1024]{0,1:T(8,128)S(1)} %copy.34) | copy-start | bytes 3145732
  99.2 11.5 %copy-start.4 = (f32[256,8,64]{2,0,1:T(8,128)}, f32[256,8,64]{2,0,1:T(8,128)S(1)}, u32[]{:S(2)}) copy-start(f32[256,8,64]{2,0,1:T(8,128)S(1)} %copy.43) | copy-start | bytes 1572868
  105.0 5.0 copy-start.37
  192.1 2.8 copy-start.19
  192.1 2.8 copy-start.29
  224.8 5.3 copy-start.17
  224.8 5.3 copy-start.41
  230.2 2.9 copy-start.18
  239.9 5.7 %copy-start.43 = (bf16[1024,1152]{1,0:T(8,128)(2,1)}, bf16[1024,1152]{1,0:T(8,128)(2,1)S(1)}, u32[]{:S(2)}) copy-start(bf16[1024,1152]{1,0:T(8,128)(2,1)S(1)} %get-tuple-element.28) | copy-start | bytes 7077892
  245.7 3.2 copy-start.44
  255.6 297.3 %reduce-scatter.3.cloned.1.call-start = ((), (), s32[]{:S(2)}) async-start(), calls=%async_computation.5 | async-start | bytes 6488064 | tf_op jit(solution)/shard_map/reduce_scatter | solution.py:457
  255.6 5.4 copy-start.45
  291.9 3.1 copy-start.22
  406.2 4.6 copy-start.8
  413.0 3.7 copy-start.28
  414.7 2.2 copy-start.3
  431.4 23.8 %copy-start.10 = (bf16[1,256,1024]{2,1,0:T(8,128)(2,1)S(1)}, bf16[1,256,1024]{2,1,0:T(8,128)(2,1)}, u32[]{:S(2)}) copy-start(bf16[1,256,1024]{2,1,0:T(8,128)(2,1)} %param.12) | copy-start | bytes 1572868
  431.4 23.8 %copy-start.24 = (bf16[256,16,64]{0,2,1:T(8,128)(2,1)S(1)}, bf16[256,16,64]{0,2,1:T(8,128)(2,1)}, u32[]{:S(2)}) copy-start(bf16[256,16,64]{0,2,1:T(8,128)(2,1)} %copy-done.23) | copy-start | bytes 1572868
  431.4 23.8 %copy-start.31 = (f32[1024]{0:T(1024)S(1)}, f32[1024]{0:T(1024)}, u32[]{:S(2)}) copy-start(f32[1024]{0:T(1024)} %param.20) | copy-start | bytes 12292
  431.4 23.8 %copy-start.34 = (f32[256]{0:T(256)S(1)}, f32[256]{0:T(256)}, u32[]{:S(2)}) copy-start(f32[256]{0:T(256)} %copy-done.33) | copy-start | bytes 3076
  455.3 4.8 copy-start.32
  516.5 4.5 copy-start.36
  517.5 38.7 %all-to-all-start = ((bf16[4,32,3456]{2,1,0:T(8,128)(2,1)}), bf16[4,32,3456]{2,1,0:T(8,128)(2,1)S(1)}, u32[]{:S(2)}, u32[]{:S(2)}) async-start(bf16[4,32,3456]{2,1,0:T(8,128)(2,1)} %bitcast.162), calls=%async_computation.2 | async-start | bytes 1769472 | tf_op jit(solution)/shard_map/all_to_all | solution.py:429
  (19 other events, 24.7 us)
Sparse Core Ops, SparseCore 0:
  11.4 77.9 all-gather.2
  91.7 133.1 all-gather.4
  255.7 168.4 reduce-scatter.4
  430.6 122.2 reduce-scatter.2

commit v3 on v2

--- a/solution.py
+++ b/solution.py
@@ -40,14 +40,14 @@
 
 
 def key_depth(columns):
-    return KBLOCK if columns <= 1024 else KBLOCK // 2
+    return KBLOCK // 2
 
 
 def forward_kernel(q_ref, kv_ref, qspot_ref, kspot_ref, out_ref, total_ref):
     query_cols = q_ref[0]
     width, columns = query_cols.shape
     depth = key_depth(columns)
-    query_spots = qspot_ref[...]
+    query_spots = qspot_ref[0]
 
     def step(block, carry):
         mixed, total = carry
@@ -76,15 +76,20 @@
     total_ref[0] = 1.0 / total
 
 
-def backward_kernel(q_ref, do_ref, kv_ref, out_ref, inv_ref, qspot_ref, kspot_ref, dq_ref, dkv_ref):
+def backward_kernel(shared, q_ref, do_ref, kv_ref, out_ref, inv_ref, qspot_ref, kspot_ref, dq_ref, dkv_ref):
     query_cols = q_ref[0]
     width, columns = query_cols.shape
     depth = key_depth(columns)
     grad_cols = do_ref[0]
-    query_spots = qspot_ref[...]
+    query_spots = qspot_ref[0]
     inverse = inv_ref[0]
     diagonal = jnp.sum(grad_cols.astype(jnp.float32) * out_ref[0], axis=0, keepdims=True)
     last = (((1,), (1,)), ((), ()))
+    fresh = pl.program_id(0) == 0 if shared else True
+
+    @pl.when(fresh)
+    def _():
+        dkv_ref[...] = jnp.zeros_like(dkv_ref)
 
     def step(block, query_grad):
         rows = pl.ds(pl.multiple_of(block * depth, depth), depth)
@@ -95,12 +100,12 @@
         probs = jnp.where(allowed, jnp.exp(scores), 0.0) * inverse
         prob_grad = jnp.dot(values, grad_cols, preferred_element_type=jnp.float32)
         score_low = (probs * (prob_grad - diagonal)).astype(jnp.bfloat16)
-        dkv_ref[rows, :width] = lax.dot_general(
+        dkv_ref[rows, :width] += lax.dot_general(
             score_low, query_cols, last, preferred_element_type=jnp.float32
-        ).astype(jnp.bfloat16)
-        dkv_ref[rows, width:] = lax.dot_general(
+        )
+        dkv_ref[rows, width:] += lax.dot_general(
             probs.astype(jnp.bfloat16), grad_cols, last, preferred_element_type=jnp.float32
-        ).astype(jnp.bfloat16)
+        )
         return query_grad + lax.dot_general(
             keys, score_low, (((0,), (0,)), ((), ())), preferred_element_type=jnp.float32
         )
@@ -130,13 +135,14 @@
 def attend(query_cols, kv_all, query_row, key_col):
     seq_rows = kv_all.shape[0]
     groups, width, columns = query_cols.shape
+    shared = kv_all.shape[1] == 2 * width
     return pl.pallas_call(
         forward_kernel,
         grid=(groups,),
         in_specs=[
             pl.BlockSpec((1, width, columns), lambda p: (p, 0, 0)),
-            pl.BlockSpec((seq_rows, 2 * width), lambda p: (0, p)),
-            pl.BlockSpec((1, columns), lambda p: (0, 0)),
+            pl.BlockSpec((seq_rows, 2 * width), lambda p: (0, 0 if shared else p)),
+            pl.BlockSpec((1, 1, columns), lambda p: (p, 0, 0)),
             pl.BlockSpec((seq_rows, 1), lambda p: (0, 0)),
         ],
         out_specs=[
@@ -159,25 +165,26 @@
 def attend_back(query_cols, grad_cols, kv_all, mixed, inverse, query_row, key_col):
     seq_rows = kv_all.shape[0]
     groups, width, columns = query_cols.shape
+    shared = kv_all.shape[1] == 2 * width
     return pl.pallas_call(
-        backward_kernel,
+        functools.partial(backward_kernel, shared),
         grid=(groups,),
         in_specs=[
             pl.BlockSpec((1, width, columns), lambda p: (p, 0, 0)),
             pl.BlockSpec((1, width, columns), lambda p: (p, 0, 0)),
-            pl.BlockSpec((seq_rows, 2 * width), lambda p: (0, p)),
+            pl.BlockSpec((seq_rows, 2 * width), lambda p: (0, 0 if shared else p)),
             pl.BlockSpec((1, width, columns), lambda p: (p, 0, 0)),
             pl.BlockSpec((1, 1, columns), lambda p: (p, 0, 0)),
-            pl.BlockSpec((1, columns), lambda p: (0, 0)),
+            pl.BlockSpec((1, 1, columns), lambda p: (p, 0, 0)),
             pl.BlockSpec((seq_rows, 1), lambda p: (0, 0)),
         ],
         out_specs=[
             pl.BlockSpec((1, width, columns), lambda p: (p, 0, 0)),
-            pl.BlockSpec((seq_rows, 2 * width), lambda p: (0, p)),
+            pl.BlockSpec((seq_rows, 2 * width), lambda p: (0, 0 if shared else p)),
         ],
         out_shape=[
             jax.ShapeDtypeStruct((groups, width, columns), jnp.float32),
-            jax.ShapeDtypeStruct((seq_rows, groups * 2 * width), jnp.bfloat16),
+            jax.ShapeDtypeStruct(kv_all.shape, jnp.float32),
         ],
         compiler_params=pltpu.CompilerParams(vmem_limit_bytes=VMEM_LIMIT),
         cost_estimate=pl.CostEstimate(
@@ -240,13 +247,14 @@
 
 
 def split_heads(cols, spans):
-    total = cols.shape[1] // 2
-    return cols.reshape(HD, 2, total).transpose(2, 1, 0).reshape(spans, total // spans, 2 * HD)
+    chunks, _, columns = cols.shape
+    rows = cols.reshape(chunks, HD, 2, columns // 2).transpose(0, 3, 2, 1)
+    return rows.reshape(spans, chunks * columns // (2 * spans), 2 * HD)
 
 
 def join_heads(rows):
-    total = rows.shape[0]
-    return rows.reshape(total, 2, HD).transpose(2, 1, 0).reshape(1, HD, 2 * total)
+    chunks = rows.shape[0] // KBLOCK
+    return rows.reshape(chunks, KBLOCK, 2, HD).transpose(0, 3, 2, 1).reshape(chunks, HD, 2 * KBLOCK)
 
 
 def weave(left, right):
@@ -304,7 +312,7 @@
     query_spots = lax.dynamic_slice_in_dim(key_spots, lax.axis_index("ctx") * tok_rows, tok_rows)
     cosines, sines = angles(query_spots)
     key_col = key_spots[:, None]
-    query_row = jnp.tile(query_spots, 4)[None, :]
+    query_row = jnp.tile(query_spots, 4 * PAIRS).reshape(PAIRS, 1, 4 * tok_rows)
 
     first_weights = lax.all_gather(
         jnp.concatenate([w_qkv, w_out.T], axis=1), ("ctx", "fsdp"), axis=0, tiled=True
@@ -327,7 +335,9 @@
     tok_f32 = tokens.reshape(tok_rows, model_width).astype(jnp.float32)
     normed, attn_pull = jax.vjp(rms_norm, tok_f32, attn_gain)
     normed_low = normed.astype(low)
-    normed_low, cot_all, ffn_rows = lax.optimization_barrier((normed_low, cot_all, ffn_rows))
+    normed_low, cot_all, ffn_rows, cosines, sines = lax.optimization_barrier(
+        (normed_low, cot_all, ffn_rows, cosines, sines)
+    )
     ffn_weights = lax.all_gather(
         ffn_rows.reshape(ways * own_rows, 3 * part), "ctx", axis=0, tiled=True
     )
@@ -347,7 +357,7 @@
     key_low = key_rot.astype(low).reshape(tok_rows, kv_width)
     query_low = query_rot.astype(low) * low(scale)
     if by_head:
-        query_row = jnp.tile(key_spots, 2)[None, :]
+        query_row = jnp.tile(key_spots.reshape(-1, 1, KBLOCK), (1, 1, 2))
         sent = jnp.concatenate(
             [
                 query_low.reshape(tok_rows, KV_HEADS, 2 * HD),
@@ -364,7 +374,7 @@
         query_cols = head_columns(query_low.reshape(tok_rows, q_width))
     mixed, inverse = attend(query_cols, kv_all, query_row, key_col)
     if by_head:
-        attended_low = exchange(split_heads(mixed[0].astype(low), span_count), "ctx", 4)
+        attended_low = exchange(split_heads(mixed.astype(low), span_count), "ctx", 4)
         attended_low = attended_low.transpose(1, 0, 2).reshape(tok_rows, q_width)
     else:
         attended_low = column_heads(mixed.astype(low), tok_rows)
@@ -412,8 +422,8 @@
     if by_head:
         sent = jnp.concatenate(
             [
-                split_heads((query_grad[0] * scale).astype(low), span_count),
-                kv_grad.reshape(span_count, tok_rows, 2 * HD),
+                split_heads((query_grad * scale).astype(low), span_count),
+                kv_grad.astype(low).reshape(span_count, tok_rows, 2 * HD),
             ],
             axis=-1,
         )
@@ -423,7 +433,7 @@
         value_sum = received[:, :, 3 * HD :].reshape(tok_rows, kv_width)
     else:
         query_sum = column_heads(query_grad * scale, tok_rows)
-        kv_sum = lax.psum_scatter(kv_grad, "ctx", scatter_dimension=0, tiled=True)
+        kv_sum = lax.psum_scatter(kv_grad.astype(low), "ctx", scatter_dimension=0, tiled=True)
         key_sum, value_sum = unweave(kv_sum)
 
     grad_ffn = lax.all_to_all(

time: 574 us -> 580 us (1.010)
  Pallas kernels: 291 us -> 302 us
  transfers between devices with their start and end apart: 5 -> 5, of which waited for: 3 -> 2; matrix products, arithmetic and copies ran while one was open for 18% -> 17% of each run, Pallas kernels for 51% -> 53%
where the time goes in v3:
time: 580 us; the launch traced here: 572 us
  Pallas kernels  302 us (52%)
  matrix products  60.6 us (10%)
  blocking collectives  57.1 us (10%)
  waiting for transfers between devices  55.2 us (10%)
  local copies, waits for them, and re-layouts  44.5 us (8%)
  other arithmetic  33 us (6%)
  between operations  15.3 us (3%)
    pallas_call x9, Pallas kernels, exchange(): pl.pallas_call(functools.partial(exchange_kernel, axis, count, spread), i...  257 us
    dot_general x14, matrix products, dot(): lax.dot_general(left, right, (((left_dim,), (right_dim,)), ((), ())), pre...  57.2 us
    psum x1, blocking collectives, body(): lax.psum((attn_gain_grad, ffn_gain_grad, query_gain_grad, key_gain_grad),...  57.1 us
    pallas_call x1, Pallas kernels, attend_back(): pl.pallas_call(functools.partial(backward_kernel, shared), grid=(groups,)...  29 us
    reduce_scatter x1, waiting for transfers between devices, body(): lax.psum_scatter(grad_first, ('ctx', 'fsdp'), scatter_dimension=0, tiled=...  28.1 us
    all_gather x1, waiting for transfers between devices, body(): lax.all_gather(jnp.concatenate([w_qkv, w_out.T], axis=1), ('ctx', 'fsdp')...  27 us
    pallas_call x1, Pallas kernels, attend(): pl.pallas_call(forward_kernel, grid=(groups,), in_specs=[pl.BlockSpec((1,...  16.6 us
  transfers between devices with their start and end apart: 5, of which 2 were waited for; matrix products, arithmetic and copies ran while one was open for 17% of the time, Pallas kernels for 53%

profile of v3, /device:TPU:0, one launch (start us, length us, event | category | flops | bytes accessed | tf_op | source)
XLA Modules:
  0.0 571.8 jit_solution(1968956205346991431)
XLA Ops:
  12.0 14.7 %shard_map.204 = bf16[4,32,3456]{2,1,0:T(8,128)(2,1)} custom-call(bf16[4,32,3456]{2,1,0:T(8,128)(2,1)} %maximum_bitcast_fusion.1.src), custom_call_target="tpu_custom_call" | custom-call | bytes 40000000 | tf_op jit(solution)/shard_map/pallas_call | solution.py:234
  26.8 31.2 %shard_map.203 = bf16[4,256,1024]{2,1,0:T(8,128)(2,1)} custom-call(bf16[256,1024]{1,0:T(8,128)(2,1)} %bitcast.148), custom_call_target="tpu_custom_call" | custom-call | bytes 40000000 | tf_op jit(solution)/shard_map/pallas_call | solution.py:234
  62.4 27.0 %all-gather.3.cloned.1.call-done = bf16[1024,3072]{1,0:T(8,128)(2,1)} async-done(((bf16[32,3072]{1,0:T(8,128)(2,1)}), bf16[1024,3072]{1,0:T(8,128)(2,1)}) %all-gather.3.cloned.1.call-update) | async-done | bytes 6291472 | tf_op jit(solution)/shard_map/all_gather | solution.py:317
  89.4 3.4 fusion.6
  95.3 2.4 copy.42
  101.3 2.5 copy.41
  104.9 2.5 copy.37
  115.0 30.3 %shard_map.205 = bf16[8,256,256]{2,1,0:T(8,128)(2,1)} custom-call(bf16[8,256,256]{2,1,0:T(8,128)(2,1)} %maximum_bitcast_fusion.src), custom_call_target="tpu_custom_call" | custom-call | bytes 40000000 | tf_op jit(solution)/shard_map/pallas_call | solution.py:234
  148.1 16.6 %shard_map.206 = (f32[4,64,1024]{2,1,0:T(8,128)S(1)}, f32[4,1,1024]{2,1,0:T(1,128)S(1)}) custom-call(bf16[4,64,1024]{2,1,0:T(8,128)(2,1)S(1)} %reshape.416.q_ref, bf16[2048,128]{1,0:T(8,128)(2,1)S(1)} %get-tuple-element.62.kv_ref, s32[4,1,1024]{2,1,0:T(1,128)S(1)} %tile.9.qspot_ref, s32[2048,1]{1,0:T(8,128)S(1)} %copy.48.kspot_ref), custom_call_target="tpu_custom_call" | custom-call | flops 2147483648 | bytes 12582912 | tf_op jit(solution)/shard_map/pallas_call | solution.py:139
  166.9 28.8 %shard_map.207 = bf16[8,256,128]{2,1,0:T(8,128)(2,1)} custom-call(bf16[8,256,128]{2,1,0:T(8,128)(2,1)} %copy.50.src), custom_call_target="tpu_custom_call" | custom-call | bytes 40000000 | tf_op jit(solution)/shard_map/pallas_call | solution.py:234
  197.0 2.7 multiply_reduce_fusion.6
  200.9 24.8 %shard_map.208 = bf16[4,256,1024]{2,1,0:T(8,128)(2,1)} custom-call(bf16[256,1024]{1,0:T(8,128)(2,1)} %multiply_convert_fusion.3.src), custom_call_target="tpu_custom_call" | custom-call | bytes 40000000 | tf_op jit(solution)/shard_map/pallas_call | solution.py:234
  225.7 5.3 fusion.10
  231.1 2.9 fusion.18
  234.0 6.9 %multiply_convert_fusion = (bf16[1024,1152]{1,0:T(8,128)(2,1)}, bf16[1024,1152]{1,0:T(8,128)(2,1)S(1)}, bf16[1024,1152]{1,0:T(8,128)(2,1)}) fusion(f32[1024,1152]{1,0:T(8,128)S(1)} %fusion.10, f32[1024,1152]{1,0:T(8,128)S(1)} %fusion.18, bf16[1024,1024]{1,0:T(8,128)(2,1)S(1)} %bitcast.141, bf16[1024,3456]{1,0:T(8,128)(2,1)S(1)} %copy-done.41), kind=kOutput, calls=%fused_computation.6 | convolution fusion | flops 2434793472 | bytes 20971520 | tf_op jit(solution)/shard_map/dot_general | solution.py:276
  240.9 5.7 convolution_convert_fusion.1
  246.6 3.2 convolution_convert_fusion.3
  249.8 3.5 convolution_convert_fusion.2
  253.3 3.4 pad_maximum_fusion
  256.8 5.4 fusion.8
  262.2 5.8 %add_convert_fusion = bf16[1024,1024]{1,0:T(8,128)(2,1)} fusion(f32[1024,1024]{1,0:T(8,128)S(1)} %fusion.8, bf16[1024,1152]{1,0:T(8,128)(2,1)S(1)} %copy-done.45, bf16[1024,3456]{1,0:T(8,128)(2,1)} %all-gather.5.cloned.1.call-done), kind=kOutput, calls=%fused_computation.12 | convolution fusion | flops 2418016256 | bytes 11010048 | tf_op jit(solution)/shard_map/dot_general | solution.py:276
  268.1 25.3 %shard_map.209 = bf16[4,256,1024]{2,1,0:T(8,128)(2,1)} custom-call(bf16[4,256,1024]{2,1,0:T(8,128)(2,1)} %bitcast.146), custom_call_target="tpu_custom_call" | custom-call | bytes 40000000 | tf_op jit(solution)/shard_map/pallas_call | solution.py:234
  301.3 31.7 %shard_map.210 = bf16[8,256,128]{2,1,0:T(8,128)(2,1)} custom-call(bf16[8,256,128]{2,1,0:T(8,128)(2,1)} %bitcast.154), custom_call_target="tpu_custom_call" | custom-call | bytes 40000000 | tf_op jit(solution)/shard_map/pallas_call | solution.py:234
  335.8 29.0 %shard_map.211 = (f32[4,64,1024]{2,1,0:T(8,128)S(1)}, f32[2048,128]{1,0:T(8,128)S(1)}) custom-call(bf16[4,64,1024]{2,1,0:T(8,128)(2,1)S(1)} %reshape.416.q_ref, bf16[4,64,1024]{2,1,0:T(8,128)(2,1)S(1)} %reshape.424.do_ref, bf16[2048,128]{1,0:T(8,128)(2,1)S(1)} %get-tuple-element.62.kv_ref, f32[4,64,1024]{2,1,0:T(8,128)} %copy-done, ...), custom_call_target="tpu_custom_call" | custom-call | flops 5368709120 | bytes 20971520 | tf_op jit(solution)/shard_map/pallas_call | solution.py:169
  367.4 45.0 %shard_map.212 = bf16[8,256,256]{2,1,0:T(8,128)(2,1)} custom-call(bf16[8,256,256]{2,1,0:T(8,128)(2,1)} %pad_maximum_fusion.2.src), custom_call_target="tpu_custom_call" | custom-call | bytes 40000000 | tf_op jit(solution)/shard_map/pallas_call | solution.py:234
  425.1 3.2 pad_maximum_fusion.1
  428.4 6.6 %fusion.20 = bf16[1024,1024]{1,0:T(8,128)(2,1)} fusion(bf16[1024,1152]{1,0:T(8,128)(2,1)} %get-tuple-element.38, bf16[1024,3456]{1,0:T(8,128)(2,1)} %all-gather.5.cloned.1.call-done), kind=kOutput, calls=%fused_computation.38 | convolution fusion | flops 2416967680 | bytes 6815744 | tf_op jit(solution)/shard_map/dot_general | solution.py:276
  435.0 24.8 %shard_map.213 = bf16[4,256,1024]{2,1,0:T(8,128)(2,1)} custom-call(bf16[4,256,1024]{2,1,0:T(8,128)(2,1)} %bitcast.147), custom_call_target="tpu_custom_call" | custom-call | bytes 40000000 | tf_op jit(solution)/shard_map/pallas_call | solution.py:234
  459.8 4.7 fusion.37
  464.5 57.1 %all-reduce.4 = (f32[1024]{0:T(1024)}, f32[1024]{0:T(1024)}, f32[64]{0:T(128)}, f32[64]{0:T(128)}) all-reduce(f32[1024]{0:T(1024)S(1)} %get-tuple-element.45, f32[1024]{0:T(1024)S(1)} %copy-done.31, f32[64]{0:T(128)S(1)} %get-tuple-element.47, f32[64]{0:T(128)S(1)} %copy-done.40), channel_id=1, replica_groups=mesh['ctx'=8,'fsdp'=4] {'ctx','fsdp'}, use_global_device_ids=true, to_apply=%region_13.14 | all-reduce | flops 2176 | bytes 17408 | tf_op jit(solution)/shard_map/psum | solution.py:475
  524.8 3.5 all-to-all-start
  530.7 28.1 %reduce-scatter.3.cloned.1.call-done = bf16[32,3072]{1,0:T(8,128)(2,1)} async-done(((bf16[1024,3072]{1,0:T(8,128)(2,1)}), bf16[32,3072]{1,0:T(8,128)(2,1)}) %reduce-scatter.3.cloned.1.call-update) | async-done | bytes 196624 | tf_op jit(solution)/shard_map/reduce_scatter | solution.py:467
  (209 shorter events, 68.0 us)
Async XLA Ops:
  7.2 82.3 %all-gather.3.cloned.1.call-start = ((), (), s32[]{:S(2)}) async-start(), calls=%async_computation.3 | async-start | bytes 6488064 | tf_op jit(solution)/shard_map/all_gather | solution.py:317
  8.9 216.8 %all-gather.5.cloned.1.call-start = ((), (), s32[]{:S(2)}) async-start(), calls=%async_computation.4 | async-start | bytes 7962624 | tf_op jit(solution)/shard_map/all_gather | solution.py:341
  12.0 46.0 %copy-start.42 = (s32[1,16]{1,0:T(1,128)S(1)}, s32[1,16]{1,0:T(1,128)}, u32[]{:S(2)}) copy-start(s32[1,16]{1,0:T(1,128)} %param.14) | copy-start | bytes 196
  12.0 46.8 %copy-start.11 = (bf16[1,256,1024]{2,1,0:T(8,128)(2,1)S(1)}, bf16[1,256,1024]{2,1,0:T(8,128)(2,1)}, u32[]{:S(2)}) copy-start(bf16[1,256,1024]{2,1,0:T(8,128)(2,1)} %param.12) | copy-start | bytes 1572868
  12.0 47.1 %copy-start.29 = (f32[1024]{0:T(1024)S(1)}, f32[1024]{0:T(1024)}, u32[]{:S(2)}) copy-start(f32[1024]{0:T(1024)} %param.20) | copy-start | bytes 12292
  26.8 32.6 %copy-start.38 = (f32[64]{0:T(128)S(1)}, f32[64]{0:T(128)}, u32[]{:S(2)}) copy-start(f32[64]{0:T(128)} %param.22) | copy-start | bytes 772
  59.3 30.2 %copy-start.17 = (bf16[256,1024]{1,0:T(8,128)(2,1)}, bf16[256,1024]{1,0:T(8,128)(2,1)S(1)}, u32[]{:S(2)}) copy-start(bf16[256,1024]{1,0:T(8,128)(2,1)S(1)} %fusion.36) | copy-start | bytes 1572868
  59.3 465.4 %reduce-scatter.5.cloned.1.call-start = ((), (), s32[]{:S(2)}) async-start(), calls=%async_computation.6 | async-start | bytes 7962624 | tf_op jit(solution)/shard_map/reduce_scatter | solution.py:405
  60.1 88.0 %copy-start.1 = (s32[2048,1]{1,0:T(8,128)}, s32[2048,1]{1,0:T(8,128)S(1)}, u32[]{:S(2)}) copy-start(s32[2048,1]{1,0:T(8,128)S(1)} %copy.48.kspot_ref) | copy-start | bytes 24580
  95.3 12.2 %copy-start.2 = (f32[256,1024]{0,1:T(8,128)}, f32[256,1024]{0,1:T(8,128)S(1)}, u32[]{:S(2)}) copy-start(f32[256,1024]{0,1:T(8,128)S(1)} %copy.34) | copy-start | bytes 3145732
  99.2 11.5 %copy-start.4 = (f32[256,8,64]{2,0,1:T(8,128)}, f32[256,8,64]{2,0,1:T(8,128)S(1)}, u32[]{:S(2)}) copy-start(f32[256,8,64]{2,0,1:T(8,128)S(1)} %copy.43) | copy-start | bytes 1572868
  104.9 5.0 copy-start.36
  197.0 2.8 copy-start.21
  197.0 2.8 copy-start.28
  199.7 96.7 %copy-start.6 = (f32[256,1024]{1,0:T(8,128)}, f32[256,1024]{1,0:T(8,128)S(1)}, u32[]{:S(2)}) copy-start(f32[256,1024]{1,0:T(8,128)S(1)} %get-tuple-element.78) | copy-start | bytes 3145732
  225.7 5.3 copy-start.19
  225.7 5.3 copy-start.41
  231.1 2.9 copy-start.20
  240.9 5.7 copy-start.43
  246.6 3.2 copy-start.44
  256.7 302.1 %reduce-scatter.3.cloned.1.call-start = ((), (), s32[]{:S(2)}) async-start(), calls=%async_computation.5 | async-start | bytes 6488064 | tf_op jit(solution)/shard_map/reduce_scatter | solution.py:467
  256.8 5.4 copy-start.45
  293.4 3.1 copy-start.24
  413.7 2.4 copy-start.10
  435.0 24.8 %copy-start.12 = (bf16[1,256,1024]{2,1,0:T(8,128)(2,1)S(1)}, bf16[1,256,1024]{2,1,0:T(8,128)(2,1)}, u32[]{:S(2)}) copy-start(bf16[1,256,1024]{2,1,0:T(8,128)(2,1)} %param.12) | copy-start | bytes 1572868
  435.0 24.8 %copy-start.30 = (f32[1024]{0:T(1024)S(1)}, f32[1024]{0:T(1024)}, u32[]{:S(2)}) copy-start(f32[1024]{0:T(1024)} %param.20) | copy-start | bytes 12292
  435.0 24.8 %copy-start.33 = (f32[256]{0:T(256)S(1)}, f32[256]{0:T(256)}, u32[]{:S(2)}) copy-start(f32[256]{0:T(256)} %copy-done.32) | copy-start | bytes 3076
  459.8 4.7 copy-start.31
  459.8 4.7 copy-start.40
  464.5 59.3 %copy-start.7 = (f32[256,1024]{1,0:T(8,128)S(1)}, f32[256,1024]{1,0:T(8,128)}, u32[]{:S(2)}) copy-start(f32[256,1024]{1,0:T(8,128)} %copy-done.6) | copy-start | bytes 3145732
  523.8 4.5 copy-start.35
  524.8 37.3 %all-to-all-start = ((bf16[4,32,3456]{2,1,0:T(8,128)(2,1)}), bf16[4,32,3456]{2,1,0:T(8,128)(2,1)S(1)}, u32[]{:S(2)}, u32[]{:S(2)}) async-start(bf16[4,32,3456]{2,1,0:T(8,128)(2,1)} %bitcast.168), calls=%async_computation.2 | async-start | bytes 1769472 | tf_op jit(solution)/shard_map/all_to_all | solution.py:439
  (19 other events, 24.6 us)
Sparse Core Ops, SparseCore 0:
  11.4 77.9 all-gather.2
  91.6 133.1 all-gather.4
  256.9 176.0 reduce-scatter.4
  439.4 119.3 reduce-scatter.2
